TPU v7x, 512 devices: a whole 4x4x16 slice. The times are simulated.
512 devices in a mesh: gx: 32 (over z, core), gy: 4 (over x), gz: 4 (over y).
Axes of the slice: x: 4, y: 4, z: 16, core: 2. Of those that a mesh axis runs over, the one named last changes fastest.
Arguments:
- source_field: float32 [3, 256, 32, 512], P(None, 'gx', 'gy', 'gz'), may hold values from -6 to 6
- cell_contrast: bfloat16 [65536, 1536], P(('gx', 'gy', 'gz')), may hold values from 0.19921875 to 2
- point_field: bfloat16 [3, 65536], P(None, ('gx', 'gy', 'gz')), may hold values from -3 to 3
- point_class: int32 [65536, 1], P(('gx', 'gy', 'gz')), may hold values from 0 to 31; in each aligned block of 128 rows (0 to 127, 128 to 255, ...) at most 8 rows name the same one
- cell_kind: int32 [65536], P(('gx', 'gy', 'gz')), may hold values from 0 to 3
- inverse_blocks: float32 [32, 4, 3, 3, 512], P('gx'), may hold values from -0.3 to 0.3
Outputs:
- newton_step: float32 [3, 256, 32, 512], P(None, 'gx', 'gy', 'gz')
- krylov_residual: float32 [3, 256, 32, 512], P(None, 'gx', 'gy', 'gz')
Inputs may be any that keep to these rules, and one draw needn't show every extreme that they name: `point_class`: among the 128 points of one device's block no class is named more than 8 times, a bound that some block reaches there.
All inputs are finite; a program needn't handle non-finite values.
Results may differ from a plain program's by a relative error of at most 0.0076.
Values may be sent and summed in bfloat16 or wider, within the bound.
A program may use at most 64 MiB of HBM per device.

v0:
```python
import math

import jax
import jax.numpy as jnp
from jax import lax
from jax.sharding import PartitionSpec as P

CELL = 8
VOX = 512
TYPES = 4
ZP = 8
ITERS = 3


kerr_scale = 0.1


def with_halo(block, sides, width):
    for axis, dim in sides:
        count = lax.axis_size(axis)
        forward = [(i, i + 1) for i in range(count - 1)]
        backward = [(target, source) for source, target in forward]
        low = lax.ppermute(
            lax.slice_in_dim(block, block.shape[dim] - width, None, axis=dim), axis, forward
        )
        high = lax.ppermute(lax.slice_in_dim(block, 0, width, axis=dim), axis, backward)
        block = jnp.concatenate([low, block, high], axis=dim)
    return block


def hartley_table():
    voxel_index = jnp.arange(VOX, dtype=jnp.int32)
    along_one = voxel_index // (CELL * CELL)
    along_two = voxel_index // CELL % CELL
    along_three = voxel_index % CELL
    phase_index = (
        along_one[:, None] * along_one[None, :]
        + along_two[:, None] * along_two[None, :]
        + along_three[:, None] * along_three[None, :]
    ) % CELL
    phase_angle = 2.0 * math.pi / CELL * phase_index.astype(jnp.float32)
    return ((jnp.cos(phase_angle) + jnp.sin(phase_angle)) / math.sqrt(VOX)).astype(jnp.bfloat16)


def cell_solve(contrast, point_values, blocks, hartley):
    row_count = contrast.shape[0]
    weights = contrast.reshape(row_count, 3, VOX).astype(jnp.float32)
    base_field = point_values.astype(jnp.float32)[:, :, None]

    def correction(polarization):
        spectrum = jnp.dot(
            polarization.reshape(row_count * 3, VOX), hartley, preferred_element_type=jnp.float32
        ).reshape(row_count, 3, VOX)
        mixed_spectrum = jnp.sum(blocks * spectrum[:, None, :, :], axis=2).astype(jnp.bfloat16)
        return jnp.dot(
            mixed_spectrum.reshape(row_count * 3, VOX), hartley, preferred_element_type=jnp.float32
        ).reshape(row_count, 3, VOX)

    local_field = base_field - correction((weights * base_field).astype(jnp.bfloat16))
    kerr_polar = (weights * local_field * (1.0 + kerr_scale * local_field * local_field)).astype(
        jnp.bfloat16
    )
    final_field = base_field - correction(kerr_polar)
    flux_mean = jnp.mean((1.0 + weights) * final_field, axis=2)
    stiffness = 0.5 + jnp.mean(weights * final_field * final_field, axis=(1, 2))
    return jnp.concatenate([flux_mean, stiffness[:, None]], axis=1)


def solve_batched(contrast, point_values, keys, library, hartley):
    return cell_solve(contrast, point_values, library[keys], hartley)


def operate(field, diagonal):
    padded = with_halo(field, (("gx", 1), ("gy", 2), ("gz", 3)), 1)
    beside = padded[:, 2:, 1:-1, 1:-1] + padded[:, :-2, 1:-1, 1:-1]
    beside = beside + padded[:, 1:-1, 2:, 1:-1] + padded[:, 1:-1, :-2, 1:-1]
    beside = beside + padded[:, 1:-1, 1:-1, 2:] + padded[:, 1:-1, 1:-1, :-2]
    return (6.0 + diagonal)[None] * field - beside


def squares(residual):
    return lax.psum(jnp.sum(residual * residual), ("gx", "gy", "gz"))


def per_device(source_field, cell_contrast, point_field, point_class, cell_kind, inverse_blocks):
    hartley = hartley_table()
    point_values = point_field.T
    library = lax.all_gather(inverse_blocks, "gx", axis=0, tiled=True)
    library = library.reshape(library.shape[0] * library.shape[1], 3, 3, VOX)
    chosen = point_class[:, 0] * TYPES + cell_kind
    summary = solve_batched(cell_contrast, point_values, chosen, library, hartley)
    extent_x = source_field.shape[1]
    extent_y = source_field.shape[2]
    extent_z = source_field.shape[3]
    blocks_z = extent_z // ZP
    stiffness_grid = jnp.broadcast_to(
        summary[:, 3].reshape(1, extent_y, blocks_z, 1), (extent_x, extent_y, blocks_z, ZP)
    ).reshape(extent_x, extent_y, extent_z)
    flux_grid = jnp.broadcast_to(
        summary[:, :3].T.reshape(3, 1, extent_y, blocks_z, 1), (3, extent_x, extent_y, blocks_z, ZP)
    ).reshape(3, extent_x, extent_y, extent_z)
    right = source_field - flux_grid
    newton_step = jnp.zeros_like(right)
    residual = right
    direction = right
    norm_now = squares(residual)
    for iteration in range(ITERS):
        image = operate(direction, stiffness_grid)
        alpha = norm_now / lax.psum(jnp.sum(direction * image), ("gx", "gy", "gz"))
        newton_step = newton_step + alpha * direction
        residual = residual - alpha * image
        norm_next = squares(residual)
        direction = residual + norm_next / norm_now * direction
        norm_now = norm_next
    return (newton_step, residual)


def solution(mesh):
    placed = (
        P(None, "gx", "gy", "gz"),
        P(("gx", "gy", "gz"), None),
        P(None, ("gx", "gy", "gz")),
        P(("gx", "gy", "gz"), None),
        P(("gx", "gy", "gz")),
        P("gx", None, None, None, None),
    )
    return jax.shard_map(
        per_device,
        mesh=mesh,
        in_specs=placed,
        out_specs=(P(None, "gx", "gy", "gz"), P(None, "gx", "gy", "gz")),
        check_vma=False,
    )
```

profile of v0, /device:TPU:1, one launch (start us, length us, event | category | flops | bytes accessed | tf_op | source)
XLA Modules:
  0.0 722.5 jit_solution(11703445166906747007)
XLA Ops:
  7.9 1.2 copy.34
  10.1 4.7 fusion.12
  14.8 1.5 copy.39
  16.4 71.8 %all-gather.2.cloned.1.call-done = f32[32,4,3,3,512]{4,1,3,2,0:T(4,128)} async-done(((f32[1,4,3,3,512]{4,1,3,2,0:T(4,128)}), f32[32,4,3,3,512]{4,1,3,2,0:T(4,128)}) %all-gather.2.cloned.1.call-update) | async-done | bytes 2359312 | tf_op jit(solution)/shard_map/all_gather | solution.py:88
  88.2 4.6 copy.45
  92.7 4.3 gather_fusion
  97.1 4.6 multiply_reduce_fusion.1
  101.7 11.6 %fusion.7 = f32[128,3,512]{2,0,1:T(8,128)} fusion(f32[128,3,512]{2,0,1:T(8,128)} %copy-done.1, s32[512]{0:T(512)S(1)} %get-tuple-element.33, s32[512]{0:T(512)S(1)} %get-tuple-element.34, s32[512]{0:T(512)S(1)} %add_select_fusion.4, bf16[128,3,512]{2,1,0:T(4,128)(2,1)} %multiply_reduce_fusion.1, f32[128,3]{0,1:T(4,128)S(1)} %convert_bitcast_fusion), kind=kOutput, calls=%fused_computation.21 | convolution fusion | flops 415039488 | bytes 1973760 | tf_op jit(solution)/shard_map/dot_general | solution.py:51
  113.3 1.7 copy.42
  115.0 3.7 multiply_reduce_fusion
  118.7 4.9 fusion.6
  124.0 2.2 collective-permute-start
  126.2 3.4 collective-permute-start.1
  129.6 0.8 collective-permute-done.1
  130.5 1.3 collective-permute-start.2
  131.8 4.0 collective-permute-start.3
  135.8 0.8 collective-permute-done.3
  136.8 3.1 collective-permute-start.5
  139.9 1.3 collective-permute-start.4
  141.5 3.6 collective-permute-done.5
  145.1 3.8 collective-permute-done.4
  148.9 0.8 multiply_reduce_fusion.7
  149.7 102.9 %all-reduce = (f32[]{:T(128)}, f32[]{:T(128)}) all-reduce(f32[]{:T(128)} %get-tuple-element.5, f32[]{:T(128)} %get-tuple-element.4), channel_id=1, replica_groups=mesh['gx'=32,'gy'=4,'gz'=4] {'gx','gy','gz'}, use_global_device_ids=true, to_apply=%region_4.5 | all-reduce | flops 2 | bytes 16 | tf_op jit(solution)/shard_map/psum | solution.py:82
  254.6 100.5 %psum.44 = f32[]{:T(128)} all-reduce(f32[]{:T(128)} %multiply_reduce_fusion.6), channel_id=1, replica_groups=mesh['gx'=32,'gy'=4,'gz'=4] {'gx','gy','gz'}, use_global_device_ids=true, to_apply=%region_9.10 | all-reduce | flops 1 | bytes 8 | tf_op jit(solution)/shard_map/psum | solution.py:82
  356.5 2.6 collective-permute-start.6
  359.1 3.0 collective-permute-start.7
  362.1 0.8 collective-permute-done.7
  362.9 1.3 collective-permute-start.8
  364.2 4.0 collective-permute-start.9
  368.2 0.8 collective-permute-done.9
  369.2 2.5 collective-permute-start.11
  371.8 1.3 collective-permute-start.10
  373.1 3.5 collective-permute-done.11
  376.5 3.8 collective-permute-done.10
  380.3 0.8 multiply_reduce_fusion.5
  381.2 101.6 %psum.45 = f32[]{:T(128)} all-reduce(f32[]{:T(128)} %get-tuple-element.12), channel_id=1, replica_groups=mesh['gx'=32,'gy'=4,'gz'=4] {'gx','gy','gz'}, use_global_device_ids=true, to_apply=%region_11.12 | all-reduce | flops 1 | bytes 8 | tf_op jit(solution)/shard_map/psum | solution.py:109
  484.8 100.4 %psum.46 = f32[]{:T(128)} all-reduce(f32[]{:T(128)} %get-tuple-element.10), channel_id=1, replica_groups=mesh['gx'=32,'gy'=4,'gz'=4] {'gx','gy','gz'}, use_global_device_ids=true, to_apply=%region_13.14 | all-reduce | flops 1 | bytes 8 | tf_op jit(solution)/shard_map/psum | solution.py:82
  586.5 2.6 collective-permute-start.12
  589.1 3.0 collective-permute-start.13
  592.9 1.3 collective-permute-start.14
  594.2 4.0 collective-permute-start.15
  598.2 0.8 collective-permute-done.15
  599.2 2.4 collective-permute-start.17
  601.6 1.3 collective-permute-start.16
  602.9 3.5 collective-permute-done.17
  606.4 3.8 collective-permute-done.16
  610.2 0.8 multiply_reduce_fusion.3
  611.0 101.6 %psum.47 = f32[]{:T(128)} all-reduce(f32[]{:T(128)} %get-tuple-element.8), channel_id=1, replica_groups=mesh['gx'=32,'gy'=4,'gz'=4] {'gx','gy','gz'}, use_global_device_ids=true, to_apply=%region_15.16 | all-reduce | flops 1 | bytes 8 | tf_op jit(solution)/shard_map/psum | solution.py:109
  (52 shorter events, 6.3 us)
Async XLA Ops:
  7.2 81.0 %all-gather.2.cloned.1.call-start = ((), (), s32[]{:S(2)}) async-start(), calls=%async_computation | async-start | bytes 2433024 | tf_op jit(solution)/shard_map/all_gather | solution.py:88
  9.3 5.5 copy-start.1
  10.1 6.3 copy-start.3
  10.1 6.3 copy-start.4
  113.3 5.4 copy-start.2
  118.7 5.3 copy-start
  124.0 5.6 collective-permute-start
  126.2 4.2 collective-permute-start.1
  130.5 5.3 collective-permute-start.2
  131.8 4.8 collective-permute-start.3
  136.8 8.3 %collective-permute-start.5 = (f32[3,10,10,1]{3,2,1,0:T(8,128)S(1)}, f32[3,10,10,1]{3,2,1,0:T(8,128)S(1)}, u32[]{:S(2)}, u32[]{:S(2)}) collective-permute-start(f32[3,10,10,1]{3,2,1,0:T(8,128)S(1)} %get-tuple-element.20), channel_id=1, source_target_pairs={{0,1},{1,2},{2,3},{4,5},{5,6},{6,7},{8,9},{9,10},{10,11},{12,13},{... | collective-permute-start | bytes 3608 | tf_op jit(solution)/shard_map/ppermute | solution.py:23
  139.9 9.0 %collective-permute-start.4 = (f32[3,10,10,1]{3,2,1,0:T(8,128)S(1)}, f32[3,10,10,1]{3,2,1,0:T(8,128)S(1)}, u32[]{:S(2)}, u32[]{:S(2)}) collective-permute-start(f32[3,10,10,1]{3,2,1,0:T(8,128)S(1)} %get-tuple-element.19), channel_id=1, source_target_pairs={{1,0},{2,1},{3,2},{5,4},{6,5},{7,6},{9,8},{10,9},{11,10},{13,12},{... | collective-permute-start | bytes 3608 | tf_op jit(solution)/shard_map/ppermute | solution.py:26
  356.5 5.6 collective-permute-start.6
  359.1 3.8 collective-permute-start.7
  362.9 5.3 collective-permute-start.8
  364.2 4.8 collective-permute-start.9
  369.2 7.3 %collective-permute-start.11 = (f32[3,10,10,1]{3,2,1,0:T(8,128)S(1)}, f32[3,10,10,1]{3,2,1,0:T(8,128)S(1)}, u32[]{:S(2)}, u32[]{:S(2)}) collective-permute-start(f32[3,10,10,1]{3,2,1,0:T(8,128)S(1)} %get-tuple-element.18), channel_id=1, source_target_pairs={{0,1},{1,2},{2,3},{4,5},{5,6},{6,7},{8,9},{9,10},{10,11},{12,13},{... | collective-permute-start | bytes 3608 | tf_op jit(solution)/shard_map/ppermute | solution.py:23
  371.8 8.6 %collective-permute-start.10 = (f32[3,10,10,1]{3,2,1,0:T(8,128)S(1)}, f32[3,10,10,1]{3,2,1,0:T(8,128)S(1)}, u32[]{:S(2)}, u32[]{:S(2)}) collective-permute-start(f32[3,10,10,1]{3,2,1,0:T(8,128)S(1)} %get-tuple-element.17), channel_id=1, source_target_pairs={{1,0},{2,1},{3,2},{5,4},{6,5},{7,6},{9,8},{10,9},{11,10},{13,12},{... | collective-permute-start | bytes 3608 | tf_op jit(solution)/shard_map/ppermute | solution.py:26
  586.5 5.6 collective-permute-start.12
  589.1 3.8 collective-permute-start.13
  592.9 5.3 collective-permute-start.14
  594.2 4.8 collective-permute-start.15
  599.2 7.2 collective-permute-start.17
  601.6 8.6 %collective-permute-start.16 = (f32[3,10,10,1]{3,2,1,0:T(8,128)S(1)}, f32[3,10,10,1]{3,2,1,0:T(8,128)S(1)}, u32[]{:S(2)}, u32[]{:S(2)}) collective-permute-start(f32[3,10,10,1]{3,2,1,0:T(8,128)S(1)} %get-tuple-element.15), channel_id=1, source_target_pairs={{1,0},{2,1},{3,2},{5,4},{6,5},{7,6},{9,8},{10,9},{11,10},{13,12},{... | collective-permute-start | bytes 3608 | tf_op jit(solution)/shard_map/ppermute | solution.py:26
Sparse Core Ops, SparseCore 0:
  10.1 78.0 all-gather.1
where the time goes:
time: 733 us; the launch traced here: 723 us
  blocking collectives  507 us (69%)
  waiting for transfers between devices  99.3 us (14%)
  starting transfers between devices  44.5 us (6%)
  between operations  21.5 us (3%)
  matrix products  21.3 us (3%)
  local copies, waits for them, and re-layouts  14.6 us (2%)
  other arithmetic  14.3 us (2%)
    psum x3, blocking collectives, squares(): return lax.psum(jnp.sum(residual * residual), ('gx', 'gy', 'gz'))  304 us
    psum x2, blocking collectives, per_device(): alpha = norm_now / lax.psum(jnp.sum(direction * image), ('gx', 'gy', 'gz'))  203 us
    all_gather x1, waiting for transfers between devices, per_device(): library = lax.all_gather(inverse_blocks, 'gx', axis=0, tiled=True)  71.8 us
    ppermute x9, starting transfers between devices, with_halo(): lax.ppermute(lax.slice_in_dim(block, block.shape[dim] - width, None, axis...  29.4 us
    dot_general x2, matrix products, correction(): jnp.dot(polarization.reshape(row_count * 3, VOX), hartley, preferred_elem...  16.3 us
    ppermute x9, waiting for transfers between devices, with_halo(): lax.ppermute(lax.slice_in_dim(block, block.shape[dim] - width, None, axis...  15.4 us
    ppermute x9, starting transfers between devices, with_halo(): lax.ppermute(lax.slice_in_dim(block, 0, width, axis=dim), axis, backward)  15.1 us
  transfers between devices with their start and end apart: 19, of which 13 were waited for; matrix products, arithmetic and copies ran while one was open for 1% of the time, Pallas kernels for 0%

commit v1 on v0

v1 whole, which is shorter than its diff:
```python
import functools
import math

import jax
import jax.numpy as jnp
import numpy as np
from jax import lax
from jax.experimental import pallas as pl
from jax.experimental.pallas import tpu as pltpu
from jax.sharding import PartitionSpec as P

CELL = 8
VOX = 512
TYPES = 4
ZP = 8
ITERS = 3
NGX = 32
NZC = 16
NP = 16
PART = 128
ROW = 9 * PART
SLAB = ROW + PART
POINTS = 128
FIELDS = 24
KERR = 0.1
SHIFT = 7.0
THETA = 2.0**-12

MESH = pl.DeviceIdType.MESH
F32 = jnp.float32
BF16 = jnp.bfloat16


def hartley_table():
    n = np.arange(VOX)
    a, b, c = n // (CELL * CELL), n // CELL % CELL, n % CELL
    phase = (np.outer(a, a) + np.outer(b, b) + np.outer(c, c)) % CELL
    angle = 2.0 * math.pi / CELL * np.arange(CELL)
    values = ((np.cos(angle) + np.sin(angle)) / math.sqrt(VOX)).astype(np.float32)
    values[np.abs(values) < 1e-6] = 0.0
    return values.astype(jnp.bfloat16)[phase]


def kernel(
    source_ref,
    contrast_ref,
    point_ref,
    class_ref,
    kind_ref,
    inverse_ref,
    hartley_ref,
    step_ref,
    residual_ref,
    slice_buf,
    column_buf,
    lib,
    blocks,
    basis,
    out_x,
    out_y,
    out_z,
    in_x,
    in_y,
    in_z,
    plane_buf,
    line_buf,
    send_one,
    recv_one,
    send_two,
    recv_two,
    send_three,
    recv_three,
    send_halo,
    recv_halo,
    send_plane,
    recv_plane,
    send_line,
    recv_line,
):
    gx, gy, gz = lax.axis_index("gx"), lax.axis_index("gy"), lax.axis_index("gz")
    chip, core = gx // 2, gx % 2
    place = gy * 4 + gz

    def on_line(target):
        return {"gx": target, "gy": gy, "gz": gz}

    def on_plane(target):
        return {"gx": gx, "gy": target // 4, "gz": target % 4}

    barrier = pltpu.get_barrier_semaphore()

    @pl.loop(1, NGX)
    def _(d):
        pl.semaphore_signal(
            barrier, inc=1, device_id=on_line(lax.rem(gx + d, NGX)), device_id_type=MESH
        )

    @pl.loop(1, NP)
    def _(d):
        pl.semaphore_signal(
            barrier, inc=1, device_id=on_plane(lax.rem(place + d, NP)), device_id_type=MESH
        )

    for i in range(3):
        for j in range(3):
            at = (i * 3 + j) * PART
            slice_buf[:, at : at + PART] = inverse_ref[
                0, gy, i, j : j + 1, pl.ds(pl.multiple_of(gz * PART, PART), PART)
            ]
    column_buf[chip] = slice_buf[...]
    pl.semaphore_wait(barrier, NGX - 1 + NP - 1)

    def one(d):
        to = lax.rem(chip + d, NZC)
        return pltpu.make_async_remote_copy(
            src_ref=slice_buf,
            dst_ref=column_buf.at[chip],
            send_sem=send_one.at[d],
            recv_sem=recv_one.at[chip],
            device_id=on_line(to * 2 + core),
            device_id_type=MESH,
        )

    def one_arrival(d):
        source = lax.rem(chip + NZC - d, NZC)
        return pltpu.make_async_remote_copy(
            src_ref=slice_buf,
            dst_ref=column_buf.at[source],
            send_sem=send_one.at[d],
            recv_sem=recv_one.at[source],
            device_id=on_line(source * 2 + core),
            device_id_type=MESH,
        )

    @pl.loop(1, NZC)
    def _(d):
        one(d).start()

    rows = lax.broadcasted_iota(jnp.int32, (8, POINTS), 0)
    point = point_ref[...].astype(F32)
    packed = jnp.zeros((8, POINTS), F32)
    for i in range(3):
        packed = jnp.where(rows == i, jnp.broadcast_to(point[i : i + 1], (8, POINTS)), packed)
    packed = jnp.where(
        rows == 3, jnp.broadcast_to(kind_ref[...].astype(F32), (8, POINTS)), packed
    )
    columns = packed.T
    base = [columns[:, i : i + 1] for i in range(3)]
    kind = columns[:, 3:4].astype(jnp.int32)
    owner = class_ref[...]
    key = kind * NGX + (owner % 2) * NZC + owner // 2
    hot = (lax.broadcasted_iota(jnp.int32, (POINTS, POINTS), 1) == key).astype(F32).astype(BF16)
    weights = [contrast_ref[:, i * VOX : (i + 1) * VOX].astype(F32) for i in range(3)]

    def spectrum_of(polar):
        return [
            jnp.dot(polar[i], hartley_ref[...], preferred_element_type=F32) for i in range(3)
        ]

    first = spectrum_of([(weights[i] * base[i]).astype(BF16) for i in range(3)])

    @pl.loop(1, NZC)
    def _(d):
        one_arrival(d).wait_recv()

    mine = (gz * 4 + gy) * 2 + core
    wide = column_buf[...].reshape(NZC, ROW)
    narrow = wide.astype(BF16)
    lib[mine, :, 0:ROW] = narrow
    rest = wide - narrow.astype(F32)
    lanes = lax.broadcasted_iota(jnp.int32, (NZC, PART), 1)
    tail = jnp.zeros((NZC, PART), F32)
    for n in range(9):
        lead = jnp.broadcast_to(rest[:, n * PART : n * PART + 1], (NZC, PART))
        tail = jnp.where(lanes == n, lead, tail)
    lib[mine, :, ROW:SLAB] = tail.astype(BF16)

    def two(d):
        return pltpu.make_async_remote_copy(
            src_ref=lib.at[mine],
            dst_ref=lib.at[mine],
            send_sem=send_two.at[d],
            recv_sem=recv_two.at[place],
            device_id=on_plane(lax.rem(place + d, NP)),
            device_id_type=MESH,
        )

    def slab_of(where):
        return (where % 4 * 4 + where // 4) * 2

    def two_arrival(d):
        source = lax.rem(place + NP - d, NP)
        at = slab_of(source) + core
        return pltpu.make_async_remote_copy(
            src_ref=lib.at[at],
            dst_ref=lib.at[at],
            send_sem=send_two.at[d],
            recv_sem=recv_two.at[source],
            device_id=on_plane(source),
            device_id_type=MESH,
        )

    def three(where, which):
        at = slab_of(where) + which
        return pltpu.make_async_remote_copy(
            src_ref=lib.at[at],
            dst_ref=lib.at[at],
            send_sem=send_three.at[where],
            recv_sem=recv_three.at[where],
            device_id=on_line(chip * 2 + 1 - core),
            device_id_type=MESH,
        )

    @pl.loop(1, NP)
    def _(d):
        two(d).start()

    three(place, core).start()

    @pl.loop(1, NP)
    def _(d):
        two_arrival(d).wait_recv()
        three(lax.rem(place + NP - d, NP), core).start()

    @pl.loop(0, NP)
    def _(w):
        three(w, 1 - core).wait_recv()

    for f in range(4):
        part = lib[f * 8 : (f + 1) * 8].reshape(POINTS, SLAB)
        chosen = jnp.dot(hot, part, preferred_element_type=F32)
        if f:
            blocks[f] = chosen[:, 0:ROW]
        else:
            lead = lax.broadcasted_iota(jnp.int32, (POINTS, PART), 1) == 0
            for n in range(9):
                tail = jnp.broadcast_to(chosen[:, ROW + n : ROW + n + 1], (POINTS, PART))
                blocks[f, :, n * PART : (n + 1) * PART] = chosen[
                    :, n * PART : (n + 1) * PART
                ] + jnp.where(lead, tail, 0.0)

    def correction(spectrum):
        mixed = []
        for i in range(3):
            parts = []
            for f in range(4):
                total = None
                for j in range(3):
                    at = (i * 3 + j) * PART
                    term = (
                        blocks[f, :, at : at + PART]
                        * spectrum[j][:, f * PART : (f + 1) * PART]
                    )
                    total = term if total is None else total + term
                parts.append(total.astype(BF16))
            mixed.append(jnp.concatenate(parts, axis=1))
        return spectrum_of(mixed)

    local = [base[i] - c for i, c in enumerate(correction(first))]
    polar = [
        (weights[i] * local[i] * (1.0 + KERR * local[i] * local[i])).astype(BF16)
        for i in range(3)
    ]
    final = [base[i] - c for i, c in enumerate(correction(spectrum_of(polar)))]
    flux = [
        jnp.sum((1.0 + weights[i]) * final[i], axis=1, keepdims=True) * (1.0 / VOX)
        for i in range(3)
    ]
    energy = sum(weights[i] * final[i] * final[i] for i in range(3))
    stiff = 0.5 + jnp.sum(energy, axis=1, keepdims=True) * (1.0 / (3 * VOX))

    q = lax.broadcasted_iota(jnp.int32, (POINTS, PART), 0)
    z = lax.broadcasted_iota(jnp.int32, (POINTS, PART), 1)
    here = (q % 16) == (z // ZP)

    def to_plane(column):
        spread = jnp.where(here, jnp.broadcast_to(column, (POINTS, PART)), 0.0)
        return jnp.sum(spread.reshape(8, 16, PART), axis=1)

    diagonal = (to_plane(stiff) + (6.0 - SHIFT)) * THETA
    for c in range(3):
        plane = to_plane(flux[c])
        for x in range(8):
            basis[0, (c * 8 + x) * 8 : (c * 8 + x + 1) * 8, :] = source_ref[c, x] - plane

    lane = lax.broadcasted_iota(jnp.int32, (8, PART), 1)
    sub = lax.broadcasted_iota(jnp.int32, (8, PART), 0)
    sides = (
        on_line(lax.rem(gx + NGX - 1, NGX)),
        on_line(lax.rem(gx + 1, NGX)),
        {"gx": gx, "gy": lax.rem(gy + 3, 4), "gz": gz},
        {"gx": gx, "gy": lax.rem(gy + 1, 4), "gz": gz},
        {"gx": gx, "gy": gy, "gz": lax.rem(gz + 3, 4)},
        {"gx": gx, "gy": gy, "gz": lax.rem(gz + 1, 4)},
    )
    out_bufs = (out_x, out_x, out_y, out_y, out_z, out_z)
    in_bufs = (in_x, in_x, in_y, in_y, in_z, in_z)

    def halo(step, side):
        low = side % 2
        return pltpu.make_async_remote_copy(
            src_ref=out_bufs[side].at[step, low],
            dst_ref=in_bufs[side].at[step, 1 - low],
            send_sem=send_halo.at[step, side],
            recv_sem=recv_halo.at[step, side - low + 1 - low],
            device_id=sides[side],
            device_id_type=MESH,
        )

    def halo_arrival(step, side):
        low = side % 2
        return pltpu.make_async_remote_copy(
            src_ref=out_bufs[side].at[step, low],
            dst_ref=in_bufs[side].at[step, low],
            send_sem=send_halo.at[step, side],
            recv_sem=recv_halo.at[step, side],
            device_id=sides[side],
            device_id_type=MESH,
        )

    def tile(level, n):
        return basis[level, n * 8 : (n + 1) * 8, :]

    def dot(a, b):
        total = tile(a, 0) * tile(b, 0)
        for n in range(1, FIELDS):
            total = total + tile(a, n) * tile(b, n)
        return jnp.sum(total, axis=0, keepdims=True)

    first_x, last_x = gx == 0, gx == NGX - 1
    first_y, last_y = gy == 0, gy == 3
    first_z, last_z = gz == 0, gz == 3
    moments = []

    for step in range(ITERS):
        low_z = jnp.zeros((8, PART), F32)
        high_z = jnp.zeros((8, PART), F32)
        for c in range(3):
            out_x[step, 0, c * 8 : (c + 1) * 8, :] = tile(step, c * 8)
            out_x[step, 1, c * 8 : (c + 1) * 8, :] = tile(step, c * 8 + 7)
        halo(step, 0).start()
        halo(step, 1).start()
        out_y[step, 0] = basis[step, pl.ds(0, FIELDS, stride=8), :]
        out_y[step, 1] = basis[step, pl.ds(7, FIELDS, stride=8), :]
        halo(step, 2).start()
        halo(step, 3).start()
        for n in range(FIELDS):
            value = tile(step, n)
            low_z = jnp.where(lane == n, pltpu.roll(value, n, 1), low_z)
            high_z = jnp.where(lane == n, pltpu.roll(value, n + 1, 1), high_z)
        out_z[step, 0] = low_z
        out_z[step, 1] = high_z
        halo(step, 4).start()
        halo(step, 5).start()
        if step:
            moments.append(dot(step - 1, step))
        moments.append(dot(step, step))
        for side in range(6):
            halo_arrival(step, side).wait_recv()
        from_low = jnp.where(first_z, 0.0, in_z[step, 0])
        from_high = jnp.where(last_z, 0.0, in_z[step, 1])
        rows_low = jnp.where(first_y, 0.0, in_y[step, 0])
        rows_high = jnp.where(last_y, 0.0, in_y[step, 1])
        for c in range(3):
            edge_low = jnp.where(first_x, 0.0, in_x[step, 0, c * 8 : (c + 1) * 8, :])
            edge_high = jnp.where(last_x, 0.0, in_x[step, 1, c * 8 : (c + 1) * 8, :])
            for x in range(8):
                n = c * 8 + x
                value = tile(step, n)
                beside = edge_low if x == 0 else tile(step, n - 1)
                beside = beside + (edge_high if x == 7 else tile(step, n + 1))
                row_low = jnp.broadcast_to(rows_low[n : n + 1], (8, PART))
                row_high = jnp.broadcast_to(rows_high[n : n + 1], (8, PART))
                beside = beside + jnp.where(sub == 0, row_low, pltpu.roll(value, 1, 0))
                beside = beside + jnp.where(sub == 7, row_high, pltpu.roll(value, 7, 0))
                side_low = jnp.broadcast_to(from_low[:, n : n + 1], (8, PART))
                side_high = jnp.broadcast_to(from_high[:, n : n + 1], (8, PART))
                beside = beside + jnp.where(lane == 0, side_low, pltpu.roll(value, 1, 1))
                beside = beside + jnp.where(
                    lane == PART - 1, side_high, pltpu.roll(value, PART - 1, 1)
                )
                basis[step + 1, n * 8 : (n + 1) * 8, :] = diagonal * value - THETA * beside
    moments.append(dot(ITERS - 1, ITERS))

    stacked = jnp.zeros((8, PART), F32)
    for k, moment in enumerate(moments):
        stacked = jnp.where(sub == k, jnp.broadcast_to(moment, (8, PART)), stacked)
    plane_buf[place] = stacked

    def plane_copy(d):
        return pltpu.make_async_remote_copy(
            src_ref=plane_buf.at[place],
            dst_ref=plane_buf.at[place],
            send_sem=send_plane.at[d],
            recv_sem=recv_plane.at[place],
            device_id=on_plane(lax.rem(place + d, NP)),
            device_id_type=MESH,
        )

    def plane_arrival(d):
        source = lax.rem(place + NP - d, NP)
        return pltpu.make_async_remote_copy(
            src_ref=plane_buf.at[source],
            dst_ref=plane_buf.at[source],
            send_sem=send_plane.at[d],
            recv_sem=recv_plane.at[source],
            device_id=on_plane(source),
            device_id_type=MESH,
        )

    def line_copy(d):
        return pltpu.make_async_remote_copy(
            src_ref=line_buf.at[gx],
            dst_ref=line_buf.at[gx],
            send_sem=send_line.at[d],
            recv_sem=recv_line.at[gx],
            device_id=on_line(lax.rem(gx + d, NGX)),
            device_id_type=MESH,
        )

    def line_arrival(d):
        source = lax.rem(gx + NGX - d, NGX)
        return pltpu.make_async_remote_copy(
            src_ref=line_buf.at[source],
            dst_ref=line_buf.at[source],
            send_sem=send_line.at[d],
            recv_sem=recv_line.at[source],
            device_id=on_line(source),
            device_id_type=MESH,
        )

    @pl.loop(1, NP)
    def _(d):
        plane_copy(d).start()

    @pl.loop(1, NP)
    def _(d):
        plane_arrival(d).wait_recv()

    line_buf[gx] = jnp.sum(plane_buf[...], axis=0)

    @pl.loop(1, NGX)
    def _(d):
        line_copy(d).start()

    @pl.loop(1, NGX)
    def _(d):
        line_arrival(d).wait_recv()

    total = jnp.sum(jnp.sum(line_buf[...], axis=0), axis=1, keepdims=True)
    m = [total[k : k + 1] for k in range(6)]

    def product(a, b):
        result = None
        for i, left in enumerate(a):
            for j, right in enumerate(b):
                term = left * (right * m[i + j])
                result = term if result is None else result + term
        return result

    unit = jnp.ones((1, 1), F32)
    now = [unit]
    course = [unit]
    taken = []
    norm = m[0]
    for step in range(ITERS):
        image = [SHIFT * course[0]]
        for k in range(1, len(course)):
            image.append(SHIFT * course[k] + (1.0 / THETA) * course[k - 1])
        image.append((1.0 / THETA) * course[-1])
        alpha = norm / product(course, image)
        taken = [
            alpha * g + (taken[k] if k < len(taken) else 0.0) for k, g in enumerate(course)
        ]
        now = [
            (now[k] if k < len(now) else 0.0) - alpha * g for k, g in enumerate(image)
        ]
        if step < ITERS - 1:
            following = product(now, now)
            beta = following / norm
            course = [
                g + (beta * course[k] if k < len(course) else 0.0) for k, g in enumerate(now)
            ]
            norm = following
    taken = [jnp.broadcast_to(g, (8, PART)) for g in taken]
    now = [jnp.broadcast_to(g, (8, PART)) for g in now]
    for n in range(FIELDS):
        values = [tile(k, n) for k in range(ITERS + 1)]
        step_ref[n // 8, n % 8] = sum(taken[k] * values[k] for k in range(ITERS))
        residual_ref[n // 8, n % 8] = sum(now[k] * values[k] for k in range(ITERS + 1))

    @pl.loop(1, NZC)
    def _(d):
        one(d).wait_send()

    @pl.loop(1, NP)
    def _(d):
        two(d).wait_send()
        plane_copy(d).wait_send()

    @pl.loop(0, NP)
    def _(w):
        three(w, core).wait_send()

    for step in range(ITERS):
        for side in range(6):
            halo(step, side).wait_send()

    @pl.loop(1, NGX)
    def _(d):
        line_copy(d).wait_send()


def per_device(source_field, cell_contrast, point_field, point_class, cell_kind, inverse_blocks):
    vmem = pl.BlockSpec(memory_space=pltpu.VMEM)
    dma = pltpu.SemaphoreType.DMA
    shape = jax.ShapeDtypeStruct(source_field.shape, F32)
    return pl.pallas_call(
        kernel,
        out_shape=(shape, shape),
        in_specs=[vmem] * 7,
        out_specs=(vmem, vmem),
        scratch_shapes=[
            pltpu.VMEM((1, ROW), F32),
            pltpu.VMEM((NZC, 1, ROW), F32),
            pltpu.VMEM((2 * NP, NZC, SLAB), BF16),
            pltpu.VMEM((4, POINTS, ROW), F32),
            pltpu.VMEM((ITERS + 1, FIELDS * 8, PART), F32),
            pltpu.VMEM((ITERS, 2, FIELDS, PART), F32),
            pltpu.VMEM((ITERS, 2, FIELDS, PART), F32),
            pltpu.VMEM((ITERS, 2, 8, PART), F32),
            pltpu.VMEM((ITERS, 2, FIELDS, PART), F32),
            pltpu.VMEM((ITERS, 2, FIELDS, PART), F32),
            pltpu.VMEM((ITERS, 2, 8, PART), F32),
            pltpu.VMEM((NP, 8, PART), F32),
            pltpu.VMEM((NGX, 8, PART), F32),
            dma((NZC,)),
            dma((NZC,)),
            dma((NP,)),
            dma((NP,)),
            dma((NP,)),
            dma((NP,)),
            dma((ITERS, 6)),
            dma((ITERS, 6)),
            dma((NP,)),
            dma((NP,)),
            dma((NGX,)),
            dma((NGX,)),
        ],
        compiler_params=pltpu.CompilerParams(
            collective_id=0, has_side_effects=True, vmem_limit_bytes=40 << 20
        ),
    )(
        source_field,
        cell_contrast,
        point_field,
        point_class,
        cell_kind.reshape(1, -1),
        inverse_blocks,
        jnp.asarray(hartley_table()),
    )


def solution(mesh):
    placed = (
        P(None, "gx", "gy", "gz"),
        P(("gx", "gy", "gz"), None),
        P(None, ("gx", "gy", "gz")),
        P(("gx", "gy", "gz"), None),
        P(("gx", "gy", "gz")),
        P("gx", None, None, None, None),
    )
    return jax.shard_map(
        per_device,
        mesh=mesh,
        in_specs=placed,
        out_specs=(P(None, "gx", "gy", "gz"), P(None, "gx", "gy", "gz")),
        check_vma=False,
    )
```

time: 733 us -> 73.2 us (0.10); the launches traced: 723 us -> 72.7 us
  blocking collectives: 507 us -> 0 us
  waiting for transfers between devices: 99.3 us -> 0 us
  Pallas kernels: 0 us -> 66.9 us
  starting transfers between devices: 44.5 us -> 0 us
  matrix products: 21.3 us -> 0 us
  between operations: 21.5 us -> 0.7 us
  other arithmetic: 14.3 us -> 0 us
  local copies, waits for them, and re-layouts: 14.6 us -> 5.06 us
    psum x5 -> x0, blocking collectives: 507 us -> none  [the longest x3 304 us: squares(): return lax.psum(jnp.sum(residual * residual), ('gx', 'gy', 'gz'))]
    all_gather x1 -> x0, waiting for transfers between devices: 71.8 us -> none  [per_device(): library = lax.all_gather(inverse_blocks, 'gx', axis=0, tiled=True)]
    pallas_call x0 -> x1, Pallas kernels: none -> 66.9 us  [per_device(): pl.pallas_call(kernel, out_shape=(shape, shape), in_specs=[vmem] * 7, out...]
    ppermute x18 -> x0, starting transfers between devices: 44.4 us -> none  [the longest x9 29.4 us: with_halo(): lax.ppermute(lax.slice_in_dim(block, block.shape[dim] - width, None, axis...]
    ppermute x18 -> x0, waiting for transfers between devices: 26.9 us -> none  [the longest x9 15.4 us: with_halo(): lax.ppermute(lax.slice_in_dim(block, block.shape[dim] - width, None, axis...]
    dot_general x3 -> x0, matrix products: 21.3 us -> none  [the longest x2 16.3 us: correction(): jnp.dot(polarization.reshape(row_count * 3, VOX), hartley, preferred_elem...]
    reduce_sum x7 -> x0, other arithmetic: 12 us -> none  [the longest x2 8.26 us: correction(): jnp.sum(blocks * spectrum[:, None, :, :], axis=2).astype(jnp.bfloat16)]
  transfers between devices with their start and end apart: 19 -> 0, of which waited for: 13 -> 0; matrix products, arithmetic and copies ran while one was open for 1% -> 0% of each run, Pallas kernels for 0% -> 0%
where the time goes in v1:
time: 73.2 us; the launch traced here: 72.7 us
  Pallas kernels  66.9 us (91%)
  local copies, waits for them, and re-layouts  5.06 us (7%)
    pallas_call x1, Pallas kernels, per_device(): pl.pallas_call(kernel, out_shape=(shape, shape), in_specs=[vmem] * 7, out...  66.9 us
    unnamed x16, local copies, waits for them, and re-layouts  5.06 us

profile of v1, /device:TPU:1, one launch (start us, length us, event | category | flops | bytes accessed | tf_op | source)
XLA Modules:
  0.0 72.7 jit_solution(4183747439131944150)
XLA Ops:
  0.6 0.0 copy-start.5
  0.6 0.6 copy-done.5
  1.3 0.1 copy.9.class_ref
  1.4 0.0 copy-start.2
  1.4 0.0 copy-start.3
  1.4 0.0 copy-start.4
  1.4 1.0 %copy.10.inverse_ref = f32[1,4,3,3,512]{4,3,2,1,0:T(4,128)S(1)} copy(f32[1,4,3,3,512]{4,1,3,2,0:T(4,128)} %param.12) | data formatting | bytes 147456 | tf_op args[5]
  2.4 0.0 copy-done.2
  2.4 0.0 copy-done.3
  2.4 0.0 copy-done.4
  2.4 0.0 copy-start
  2.4 1.0 %copy-done = bf16[512,512]{1,0:T(8,128)(2,1)S(1)} copy-done((bf16[512,512]{1,0:T(8,128)(2,1)S(1)}, bf16[512,512]{1,0:T(8,128)(2,1)}, u32[]{:S(2)}) %copy-start) | copy-done | bytes 524312
  3.5 0.0 copy-start.1
  3.5 1.0 %copy-done.1 = bf16[128,1536]{1,0:T(8,128)(2,1)S(1)} copy-done((bf16[128,1536]{1,0:T(8,128)(2,1)S(1)}, bf16[128,1536]{1,0:T(8,128)(2,1)}, u32[]{:S(2)}) %copy-start.1) | copy-done | bytes 393240
  4.5 66.9 %shard_map.86 = (f32[3,8,8,128]{3,2,1,0:T(8,128)S(1)}, f32[3,8,8,128]{3,2,1,0:T(8,128)S(1)}) custom-call(f32[3,8,8,128]{3,2,1,0:T(8,128)S(1)} %copy-done.2, bf16[128,1536]{1,0:T(8,128)(2,1)S(1)} %copy-done.1, bf16[3,128]{1,0:T(4,128)(2,1)S(1)} %copy-done.3, s32[128,1]{1,0:T(8,128)S(1)} %copy.9.class_ref, s32[1,128]{1,0:T(1,128)S(1)} %bitcast.1, ...), custom_call_target="tpu_custom_call" | custom-call | tf_op jit(solution)/shard_map/pallas_call | solution.py:518
  71.4 0.6 copy.13
  72.0 0.6 copy.14
Async XLA Ops:
  0.6 0.7 copy-start.5
  1.4 1.0 %copy-start.2 = (f32[3,8,8,128]{3,2,1,0:T(8,128)S(1)}, f32[3,8,8,128]{3,2,1,0:T(8,128)}, u32[]{:S(2)}) copy-start(f32[3,8,8,128]{3,2,1,0:T(8,128)} %source_ref.1) | copy-start | bytes 294916
  1.4 1.0 %copy-start.3 = (bf16[3,128]{1,0:T(4,128)(2,1)S(1)}, bf16[3,128]{1,0:T(4,128)(2,1)}, u32[]{:S(2)}) copy-start(bf16[3,128]{1,0:T(4,128)(2,1)} %point_ref.1) | copy-start | bytes 2308
  1.4 1.0 %copy-start.4 = (s32[128]{0:T(128)S(1)}, s32[128]{0:T(128)}, u32[]{:S(2)}) copy-start(s32[128]{0:T(128)} %param.11) | copy-start | bytes 1540
  2.4 1.0 %copy-start = (bf16[512,512]{1,0:T(8,128)(2,1)S(1)}, bf16[512,512]{1,0:T(8,128)(2,1)}, u32[]{:S(2)}) copy-start(bf16[512,512]{1,0:T(8,128)(2,1)} %constant.2.clone.hartley_ref) | copy-start | bytes 1572868
  3.5 1.0 %copy-start.1 = (bf16[128,1536]{1,0:T(8,128)(2,1)S(1)}, bf16[128,1536]{1,0:T(8,128)(2,1)}, u32[]{:S(2)}) copy-start(bf16[128,1536]{1,0:T(8,128)(2,1)} %contrast_ref.1) | copy-start | bytes 1179652

commit v2 on v1

v2 whole, which is shorter than its diff:
```python
import functools
import math

import jax
import jax.numpy as jnp
import numpy as np
from jax import lax
from jax.experimental import pallas as pl
from jax.experimental.pallas import tpu as pltpu
from jax.sharding import PartitionSpec as P

CELL = 8
VOX = 512
TYPES = 4
ZP = 8
ITERS = 3
NGX = 32
NZC = 16
NP = 16
OWN = 3
PART = 128
ROW = 9 * PART
SLAB = ROW + PART
POINTS = 128
FIELDS = 24
KERR = 0.1
SHIFT = 7.0
THETA = 2.0**-12

MESH = pl.DeviceIdType.MESH
F32 = jnp.float32
BF16 = jnp.bfloat16


def hartley_table():
    n = np.arange(VOX)
    a, b, c = n // (CELL * CELL), n // CELL % CELL, n % CELL
    phase = (np.outer(a, a) + np.outer(b, b) + np.outer(c, c)) % CELL
    angle = 2.0 * math.pi / CELL * np.arange(CELL)
    values = ((np.cos(angle) + np.sin(angle)) / math.sqrt(VOX)).astype(np.float32)
    values[np.abs(values) < 1e-6] = 0.0
    return values.astype(jnp.bfloat16)[phase]


def kernel(
    source_hbm,
    contrast_hbm,
    point_hbm,
    class_hbm,
    kind_hbm,
    inverse_hbm,
    hartley_hbm,
    level_0,
    level_1,
    level_2,
    level_3,
    weight_0,
    weight_1,
    weight_2,
    weight_3,
    weight_4,
    weight_5,
    weight_6,
    source_ref,
    contrast_ref,
    point_ref,
    class_ref,
    kind_ref,
    inverse_ref,
    hartley_ref,
    slice_buf,
    column_buf,
    lib,
    blocks,
    out_halo,
    in_halo,
    plane_buf,
    line_buf,
    load_sems,
    send_one,
    recv_one,
    send_two,
    recv_two,
    send_three,
    recv_three,
    send_halo,
    recv_halo,
    send_sum,
    recv_sum,
):
    gx, gy, gz = lax.axis_index("gx"), lax.axis_index("gy"), lax.axis_index("gz")
    chip, core = gx // 2, gx % 2
    place = gy * 4 + gz
    basis = (level_0, level_1, level_2, level_3)
    weights_out = (weight_0, weight_1, weight_2, weight_3, weight_4, weight_5, weight_6)

    def on_line(target):
        return {"gx": target, "gy": gy, "gz": gz}

    def on_plane(target):
        return {"gx": gx, "gy": target // 4, "gz": target % 4}

    barrier = pltpu.get_barrier_semaphore()
    for d in sorted(range(1, NGX), key=lambda d: -min(d, NGX - d)):
        pl.semaphore_signal(
            barrier, inc=1, device_id=on_line(lax.rem(gx + d, NGX)), device_id_type=MESH
        )
    for d in range(1, NP):
        pl.semaphore_signal(
            barrier, inc=1, device_id=on_plane(lax.rem(place + d, NP)), device_id_type=MESH
        )

    loads = [
        pltpu.make_async_copy(
            inverse_hbm.at[:, :, pl.ds(pl.multiple_of(gz * PART, PART), PART)],
            inverse_ref,
            load_sems.at[0],
        )
    ]
    pairs = (
        (point_hbm, point_ref),
        (class_hbm, class_ref),
        (kind_hbm, kind_ref),
        (contrast_hbm, contrast_ref),
        (hartley_hbm, hartley_ref),
        (source_hbm, source_ref),
    )
    for n, (origin, goal) in enumerate(pairs):
        loads.append(pltpu.make_async_copy(origin, goal, load_sems.at[n + 1]))
    for load in loads:
        load.start()
    loads[0].wait()

    for n in range(9):
        slice_buf[:, n * PART : (n + 1) * PART] = inverse_ref[n, pl.ds(gy, 1), :]
    column_buf[OWN] = slice_buf[...]

    for load in loads[1:]:
        load.wait()
    rows = lax.broadcasted_iota(jnp.int32, (8, POINTS), 0)
    point = point_ref[...].astype(F32)
    packed = jnp.zeros((8, POINTS), F32)
    entries = [point[i : i + 1] for i in range(3)]
    entries += [kind_ref[...].astype(F32), class_ref[...].astype(F32)]
    for i, entry in enumerate(entries):
        packed = jnp.where(rows == i, jnp.broadcast_to(entry, (8, POINTS)), packed)
    columns = packed.T
    base = [columns[:, i : i + 1] for i in range(3)]
    kind = columns[:, 3:4].astype(jnp.int32)
    owner = columns[:, 4:5].astype(jnp.int32)
    away = (owner // 2 - chip + OWN + NZC) % NZC
    key = (away // 8) * 64 + (owner % 2) * 32 + kind * 8 + away % 8
    hot = (lax.broadcasted_iota(jnp.int32, (POINTS, POINTS), 1) == key).astype(F32).astype(BF16)
    weights = [contrast_ref[:, i * VOX : (i + 1) * VOX].astype(F32) for i in range(3)]

    def spectrum_of(polar):
        return [
            jnp.dot(polar[i], hartley_ref[...], preferred_element_type=F32) for i in range(3)
        ]

    first = spectrum_of([(weights[i] * base[i]).astype(BF16) for i in range(3)])

    pl.semaphore_wait(barrier, NGX - 1 + NP - 1)

    def one(d):
        slot = (OWN - d) % NZC
        return pltpu.make_async_remote_copy(
            src_ref=slice_buf,
            dst_ref=column_buf.at[slot],
            send_sem=send_one,
            recv_sem=recv_one.at[slot // 8],
            device_id=on_line(lax.rem(chip + d, NZC) * 2 + core),
            device_id_type=MESH,
        )

    for d in sorted(range(1, NZC), key=lambda d: -min(d, NZC - d)):
        one(d).start()

    def drain(region, send_sem, recv_sem):
        return pltpu.make_async_remote_copy(
            src_ref=region,
            dst_ref=region,
            send_sem=send_sem,
            recv_sem=recv_sem,
            device_id=on_line(chip * 2 + 1 - core),
            device_id_type=MESH,
        )

    def two(half, d):
        at = lib.at[half, core, place]
        return pltpu.make_async_remote_copy(
            src_ref=at,
            dst_ref=at,
            send_sem=send_two.at[half],
            recv_sem=recv_two.at[half],
            device_id=on_plane(lax.rem(place + d, NP)),
            device_id_type=MESH,
        )

    def three(half, which):
        return drain(lib.at[half, which], send_three.at[half], recv_three.at[half])

    lanes = lax.broadcasted_iota(jnp.int32, (8, PART), 1)
    for half in range(2):
        count = 7 if half == 0 else 8
        drain(column_buf.at[pl.ds(half * 8, count)], send_one, recv_one.at[half]).wait_recv()
        wide = column_buf[half * 8 : (half + 1) * 8].reshape(8, ROW)
        narrow = wide.astype(BF16)
        lib[half, core, place, :, 0:ROW] = narrow
        rest = wide - narrow.astype(F32)
        tail = jnp.zeros((8, PART), F32)
        for n in range(9):
            lead = jnp.broadcast_to(rest[:, n * PART : n * PART + 1], (8, PART))
            tail = jnp.where(lanes == n, lead, tail)
        lib[half, core, place, :, ROW:SLAB] = tail.astype(BF16)
        for d in range(1, NP):
            two(half, d).start()

    for half in range(2):
        region = lib.at[half, core, pl.ds(0, NP - 1)]
        drain(region, send_two.at[half], recv_two.at[half]).wait_recv()
        three(half, core).start()
    for half in range(2):
        three(half, 1 - core).wait_recv()

    for f in range(4):
        part = jnp.concatenate(
            [lib[half, c, k * 4 + f] for half in range(2) for c in range(2) for k in range(4)],
            axis=0,
        )
        chosen = jnp.dot(hot, part, preferred_element_type=F32)
        if f:
            blocks[f] = chosen[:, 0:ROW]
        else:
            lead = lax.broadcasted_iota(jnp.int32, (POINTS, PART), 1) == 0
            for n in range(9):
                tail = jnp.broadcast_to(chosen[:, ROW + n : ROW + n + 1], (POINTS, PART))
                blocks[f, :, n * PART : (n + 1) * PART] = chosen[
                    :, n * PART : (n + 1) * PART
                ] + jnp.where(lead, tail, 0.0)

    def correction(spectrum):
        mixed = []
        for i in range(3):
            parts = []
            for f in range(4):
                total = None
                for j in range(3):
                    at = (i * 3 + j) * PART
                    term = (
                        blocks[f, :, at : at + PART]
                        * spectrum[j][:, f * PART : (f + 1) * PART]
                    )
                    total = term if total is None else total + term
                parts.append(total.astype(BF16))
            mixed.append(jnp.concatenate(parts, axis=1))
        return spectrum_of(mixed)

    local = [base[i] - c for i, c in enumerate(correction(first))]
    polar = [
        (weights[i] * local[i] * (1.0 + KERR * local[i] * local[i])).astype(BF16)
        for i in range(3)
    ]
    final = [base[i] - c for i, c in enumerate(correction(spectrum_of(polar)))]
    flux = [
        jnp.sum((1.0 + weights[i]) * final[i], axis=1, keepdims=True) * (1.0 / VOX)
        for i in range(3)
    ]
    energy = sum(weights[i] * final[i] * final[i] for i in range(3))
    stiff = 0.5 + jnp.sum(energy, axis=1, keepdims=True) * (1.0 / (3 * VOX))

    q = lax.broadcasted_iota(jnp.int32, (POINTS, PART), 0)
    z = lax.broadcasted_iota(jnp.int32, (POINTS, PART), 1)
    here = (q % 16) == (z // ZP)

    def to_plane(column):
        spread = jnp.where(here, jnp.broadcast_to(column, (POINTS, PART)), 0.0)
        return jnp.sum(spread.reshape(8, 16, PART), axis=1)

    diagonal = (to_plane(stiff) + (6.0 - SHIFT)) * THETA
    for c in range(3):
        plane = to_plane(flux[c])
        for x in range(8):
            basis[0][(c * 8 + x) * 8 : (c * 8 + x + 1) * 8, :] = source_ref[c, x] - plane

    lane = lax.broadcasted_iota(jnp.int32, (8, PART), 1)
    sub = lax.broadcasted_iota(jnp.int32, (8, PART), 0)
    sides = (
        on_line(lax.rem(gx + NGX - 1, NGX)),
        on_line(lax.rem(gx + 1, NGX)),
        {"gx": gx, "gy": lax.rem(gy + 3, 4), "gz": gz},
        {"gx": gx, "gy": lax.rem(gy + 1, 4), "gz": gz},
        {"gx": gx, "gy": gy, "gz": lax.rem(gz + 3, 4)},
        {"gx": gx, "gy": gy, "gz": lax.rem(gz + 1, 4)},
    )
    starts = (0, FIELDS, 2 * FIELDS, 3 * FIELDS, 4 * FIELDS, 4 * FIELDS + 8)
    sizes = (FIELDS, FIELDS, FIELDS, FIELDS, 8, 8)

    def halo(step, side):
        goal = side + 1 - 2 * (side % 2)
        return pltpu.make_async_remote_copy(
            src_ref=out_halo.at[step, pl.ds(starts[side], sizes[side])],
            dst_ref=in_halo.at[step, pl.ds(starts[goal], sizes[goal])],
            send_sem=send_halo,
            recv_sem=recv_halo.at[step],
            device_id=sides[side],
            device_id_type=MESH,
        )

    def tile(level, n):
        return basis[level][n * 8 : (n + 1) * 8, :]

    def dot(a, b):
        total = tile(a, 0) * tile(b, 0)
        for n in range(1, FIELDS):
            total = total + tile(a, n) * tile(b, n)
        return jnp.sum(jnp.sum(total, axis=0, keepdims=True), axis=1, keepdims=True)

    keep = [
        jnp.where(edge, 0.0, -THETA)
        for edge in (gx == 0, gx == NGX - 1, gy == 0, gy == 3, gz == 0, gz == 3)
    ]
    moments = []

    for step in range(ITERS):
        for c in range(3):
            at = c * 8
            out_halo[step, starts[0] + at : starts[0] + at + 8, :] = tile(step, at)
            out_halo[step, starts[1] + at : starts[1] + at + 8, :] = tile(step, at + 7)
        halo(step, 0).start()
        halo(step, 1).start()
        faces = jnp.zeros((8, PART), F32)
        for n in range(FIELDS):
            turned = pltpu.roll(tile(step, n), 2 * n + 1, 1)
            faces = jnp.where(lane // 2 == n, turned, faces)
        out_halo[step, starts[4] : starts[4] + 8, :] = faces
        out_halo[step, starts[5] : starts[5] + 8, :] = faces
        halo(step, 4).start()
        halo(step, 5).start()
        out_halo[step, starts[2] : starts[3], :] = basis[step][pl.ds(0, FIELDS, stride=8), :]
        out_halo[step, starts[3] : starts[4], :] = basis[step][pl.ds(7, FIELDS, stride=8), :]
        halo(step, 2).start()
        halo(step, 3).start()
        for n in range(FIELDS):
            value = tile(step, n)
            beside = jnp.where(sub == 0, 0.0, pltpu.roll(value, 1, 0))
            beside = beside + jnp.where(sub == 7, 0.0, pltpu.roll(value, 7, 0))
            beside = beside + jnp.where(lane == 0, 0.0, pltpu.roll(value, 1, 1))
            beside = beside + jnp.where(lane == PART - 1, 0.0, pltpu.roll(value, PART - 1, 1))
            if n % 8:
                beside = beside + tile(step, n - 1)
            if n % 8 < 7:
                beside = beside + tile(step, n + 1)
            basis[step + 1][n * 8 : (n + 1) * 8, :] = diagonal * value - THETA * beside
        if step:
            moments.append(dot(step - 1, step))
        moments.append(dot(step, step))
        drain(in_halo.at[step], send_halo, recv_halo.at[step]).wait_recv()
        low = in_halo[step, starts[4] : starts[4] + 8, :] * keep[4]
        high = in_halo[step, starts[5] : starts[5] + 8, :] * keep[5]
        both = jnp.where(lane % 2 == 0, low, pltpu.roll(high, PART - 2, 1))
        for n in range(FIELDS):
            turned = pltpu.roll(both, (PART - 2 * n) % PART, 1)
            more = jnp.where((lane == 0) | (lane == PART - 1), turned, 0.0)
            row_low = in_halo[step, starts[2] + n : starts[2] + n + 1, :] * keep[2]
            row_high = in_halo[step, starts[3] + n : starts[3] + n + 1, :] * keep[3]
            more = more + jnp.where(sub == 0, jnp.broadcast_to(row_low, (8, PART)), 0.0)
            more = more + jnp.where(sub == 7, jnp.broadcast_to(row_high, (8, PART)), 0.0)
            at = n // 8 * 8
            if n % 8 == 0:
                more = more + in_halo[step, starts[0] + at : starts[0] + at + 8, :] * keep[0]
            if n % 8 == 7:
                more = more + in_halo[step, starts[1] + at : starts[1] + at + 8, :] * keep[1]
            basis[step + 1][n * 8 : (n + 1) * 8, :] += more
    moments.append(dot(ITERS - 1, ITERS))

    row = lax.broadcasted_iota(jnp.int32, (1, PART), 1)
    packed = jnp.zeros((1, PART), F32)
    for k, moment in enumerate(moments):
        packed = jnp.where(row == k, moment, packed)

    def all_sum(value, buf, n, turn, device_of):
        buf[0] = value

        def copy(d):
            return pltpu.make_async_remote_copy(
                src_ref=buf.at[0],
                dst_ref=buf.at[n - d],
                send_sem=send_sum.at[turn],
                recv_sem=recv_sum.at[turn],
                device_id=device_of(d),
                device_id_type=MESH,
            )

        for d in sorted(range(1, n), key=lambda d: -min(d, n - d)):
            copy(d).start()
        arrived = drain(buf.at[pl.ds(1, n - 1)], send_sum.at[turn], recv_sum.at[turn])
        arrived.wait_recv()
        return jnp.sum(buf[...], axis=0)

    packed = all_sum(packed, plane_buf, NP, 0, lambda d: on_plane(lax.rem(place + d, NP)))
    total = all_sum(packed, line_buf, NGX, 1, lambda d: on_line(lax.rem(gx + d, NGX)))
    m = [total[:, k : k + 1] for k in range(6)]

    def product(a, b):
        result = None
        for i, left in enumerate(a):
            for j, right in enumerate(b):
                term = left * (right * m[i + j])
                result = term if result is None else result + term
        return result

    unit = jnp.ones((1, 1), F32)
    now = [unit]
    course = [unit]
    taken = []
    norm = m[0]
    for step in range(ITERS):
        image = [SHIFT * course[0]]
        for k in range(1, len(course)):
            image.append(SHIFT * course[k] + (1.0 / THETA) * course[k - 1])
        image.append((1.0 / THETA) * course[-1])
        alpha = norm / product(course, image)
        taken = [
            alpha * g + (taken[k] if k < len(taken) else 0.0) for k, g in enumerate(course)
        ]
        now = [
            (now[k] if k < len(now) else 0.0) - alpha * g for k, g in enumerate(image)
        ]
        if step < ITERS - 1:
            following = product(now, now)
            beta = following / norm
            course = [
                g + (beta * course[k] if k < len(course) else 0.0) for k, g in enumerate(now)
            ]
            norm = following
    for k, g in enumerate(taken + now):
        weights_out[k][...] = jnp.broadcast_to(g, (1, PART))

    drain(column_buf.at[pl.ds(0, NZC - 1)], send_one, recv_one.at[0]).wait_send()
    for half in range(2):
        region = lib.at[half, core, pl.ds(0, NP - 1)]
        drain(region, send_two.at[half], recv_two.at[half]).wait_send()
        three(half, core).wait_send()
    drain(out_halo, send_halo, recv_halo.at[0]).wait_send()
    drain(plane_buf.at[pl.ds(1, NP - 1)], send_sum.at[0], recv_sum.at[0]).wait_send()
    drain(line_buf.at[pl.ds(1, NGX - 1)], send_sum.at[1], recv_sum.at[1]).wait_send()


def per_device(source_field, cell_contrast, point_field, point_class, cell_kind, inverse_blocks):
    vmem = pl.BlockSpec(memory_space=pltpu.VMEM)
    dma = pltpu.SemaphoreType.DMA
    results = pl.pallas_call(
        kernel,
        out_shape=[jax.ShapeDtypeStruct((FIELDS * 8, PART), F32)] * (ITERS + 1)
        + [jax.ShapeDtypeStruct((1, PART), F32)] * (2 * ITERS + 1),
        in_specs=[pl.BlockSpec(memory_space=pltpu.HBM)] * 7,
        out_specs=[vmem] * (3 * ITERS + 2),
        scratch_shapes=[
            pltpu.VMEM(source_field.shape, F32),
            pltpu.VMEM(cell_contrast.shape, BF16),
            pltpu.VMEM(point_field.shape, BF16),
            pltpu.VMEM((1, POINTS), jnp.int32),
            pltpu.VMEM((1, POINTS), jnp.int32),
            pltpu.VMEM((9, TYPES, PART), F32),
            pltpu.VMEM((VOX, VOX), BF16),
            pltpu.VMEM((1, ROW), F32),
            pltpu.VMEM((NZC, 1, ROW), F32),
            pltpu.VMEM((2, 2, NP, 8, SLAB), BF16),
            pltpu.VMEM((4, POINTS, ROW), F32),
            pltpu.VMEM((ITERS, 4 * FIELDS + 16, PART), F32),
            pltpu.VMEM((ITERS, 4 * FIELDS + 16, PART), F32),
            pltpu.VMEM((NP, 1, PART), F32),
            pltpu.VMEM((NGX, 1, PART), F32),
            dma((7,)),
            dma,
            dma((2,)),
            dma((2,)),
            dma((2,)),
            dma((2,)),
            dma((2,)),
            dma,
            dma((ITERS,)),
            dma((2,)),
            dma((2,)),
        ],
        compiler_params=pltpu.CompilerParams(
            collective_id=0, has_side_effects=True, vmem_limit_bytes=40 << 20
        ),
    )(
        *[
            pltpu.with_memory_space_constraint(value, pltpu.HBM)
            for value in (
                source_field,
                cell_contrast,
                point_field,
                point_class.reshape(1, -1),
                cell_kind.reshape(1, -1),
                inverse_blocks.transpose(0, 2, 3, 1, 4).reshape(9, TYPES, VOX),
                jnp.asarray(hartley_table()),
            )
        ]
    )
    shape = source_field.shape
    fields = [field.reshape(shape) for field in results[: ITERS + 1]]
    weights = [weight.reshape(PART) for weight in results[ITERS + 1 :]]
    newton_step = sum(weights[k] * fields[k] for k in range(ITERS))
    residual = sum(weights[ITERS + k] * fields[k] for k in range(ITERS + 1))
    return newton_step, residual


def solution(mesh):
    placed = (
        P(None, "gx", "gy", "gz"),
        P(("gx", "gy", "gz"), None),
        P(None, ("gx", "gy", "gz")),
        P(("gx", "gy", "gz"), None),
        P(("gx", "gy", "gz")),
        P("gx", None, None, None, None),
    )
    return jax.shard_map(
        per_device,
        mesh=mesh,
        in_specs=placed,
        out_specs=(P(None, "gx", "gy", "gz"), P(None, "gx", "gy", "gz")),
        check_vma=False,
    )
```

time: 73.2 us -> 58.2 us (0.80)
  Pallas kernels: 66.9 us -> 56.7 us
  local copies, waits for them, and re-layouts: 5.06 us -> 0 us
    pallas_call x1, Pallas kernels: 66.9 us -> 56.7 us  [per_device(): pl.pallas_call(kernel, out_shape=[jax.ShapeDtypeStruct((FIELDS * 8, PART)...]
    unnamed x16 -> x0, local copies, waits for them, and re-layouts: 5.06 us -> none
where the time goes in v2:
time: 58.2 us; the launch traced here: 58.1 us
  Pallas kernels  56.7 us (97%)
  other arithmetic  0.72 us (1%)
  between operations  0.64 us (1%)
    pallas_call x1, Pallas kernels, per_device(): pl.pallas_call(kernel, out_shape=[jax.ShapeDtypeStruct((FIELDS * 8, PART)...  56.7 us

profile of v2, /device:TPU:1, one launch (start us, length us, event | category | flops | bytes accessed | tf_op | source)
XLA Modules:
  0.0 58.1 jit_solution(7130572448699913656)
XLA Ops:
  0.6 56.7 %shard_map.86 = (f32[192,128]{1,0:T(8,128)S(1)}, f32[192,128]{1,0:T(8,128)S(1)}, f32[192,128]{1,0:T(8,128)S(1)}, f32[192,128]{1,0:T(8,128)S(1)}, f32[1,128]{1,0:...) custom-call(f32[3,8,8,128]{3,2,1,0:T(8,128)} %source_hbm.1, ...), custom_call_target="tpu_custom_call" | custom-call | tf_op jit(solution)/shard_map/pallas_call | solution.py:453
  57.3 0.7 %multiply_add_fusion = (f32[3,8,8,128]{3,2,1,0:T(8,128)}, f32[3,8,8,128]{3,2,1,0:T(8,128)}) fusion(f32[3,8,8,128]{3,2,1,0:T(8,128)S(1)} %bitcast.19, f32[3,8,8,128]{3,2,1,0:T(8,128)S(1)} %bitcast.18, f32[3,8,8,128]{3,2,1,0:T(8,128)S(1)} %bitcast.17, f32[3,8,8,128]{3,2,1,0:T(8,128)S(1)} %bitcast.16, f32[128]{0:T(128)S(1)} %bitcast.26, f32[128]{0:T(128)S(1)} %bitcast.25, ...), kind=kLoop, calls=%fused_computation | loop fusion | flops 294912 | bytes 593408 | tf_op jit(solution)/shard_map/add | solution.py:508

commit v3 on v2

--- a/solution.py
+++ b/solution.py
@@ -18,9 +18,11 @@
 NZC = 16
 NP = 16
 OWN = 3
+REACH = 4
 PART = 128
 ROW = 9 * PART
 SLAB = ROW + PART
+SPLIT = SLAB // 2
 POINTS = 128
 FIELDS = 24
 KERR = 0.1
@@ -101,14 +103,20 @@
         return {"gx": gx, "gy": target // 4, "gz": target % 4}
 
     barrier = pltpu.get_barrier_semaphore()
-    for d in sorted(range(1, NGX), key=lambda d: -min(d, NGX - d)):
-        pl.semaphore_signal(
-            barrier, inc=1, device_id=on_line(lax.rem(gx + d, NGX)), device_id_type=MESH
-        )
+    near = [d for reach in range(REACH, 0, -1) for d in (reach, NZC - reach)]
+
+    def chip_at(d):
+        return on_line(lax.rem(chip + d, NZC) * 2 + core)
+
+    for d in near:
+        pl.semaphore_signal(barrier, inc=1, device_id=chip_at(d), device_id_type=MESH)
     for d in range(1, NP):
         pl.semaphore_signal(
             barrier, inc=1, device_id=on_plane(lax.rem(place + d, NP)), device_id_type=MESH
         )
+    pl.semaphore_signal(
+        barrier, inc=1, device_id=on_line(chip * 2 + 1 - core), device_id_type=MESH
+    )
 
     loads = [
         pltpu.make_async_copy(
@@ -149,8 +157,9 @@
     kind = columns[:, 3:4].astype(jnp.int32)
     owner = columns[:, 4:5].astype(jnp.int32)
     away = (owner // 2 - chip + OWN + NZC) % NZC
-    key = (away // 8) * 64 + (owner % 2) * 32 + kind * 8 + away % 8
-    hot = (lax.broadcasted_iota(jnp.int32, (POINTS, POINTS), 1) == key).astype(F32).astype(BF16)
+    key = (away // 8) * 128 + (owner % 2) * 64 + kind * 16 + away % 8
+    depth = lax.broadcasted_iota(jnp.int32, (POINTS, 2 * POINTS), 1)
+    hot = [(depth == key + 8 * turn).astype(F32).astype(BF16) for turn in range(2)]
     weights = [contrast_ref[:, i * VOX : (i + 1) * VOX].astype(F32) for i in range(3)]
 
     def spectrum_of(polar):
@@ -160,21 +169,30 @@
 
     first = spectrum_of([(weights[i] * base[i]).astype(BF16) for i in range(3)])
 
-    pl.semaphore_wait(barrier, NGX - 1 + NP - 1)
+    pl.semaphore_wait(barrier, 2 * REACH + NP)
 
     def one(d):
-        slot = (OWN - d) % NZC
         return pltpu.make_async_remote_copy(
             src_ref=slice_buf,
-            dst_ref=column_buf.at[slot],
-            send_sem=send_one,
-            recv_sem=recv_one.at[slot // 8],
-            device_id=on_line(lax.rem(chip + d, NZC) * 2 + core),
+            dst_ref=column_buf.at[(OWN - d) % NZC],
+            send_sem=send_one.at[0],
+            recv_sem=recv_one.at[0],
+            device_id=chip_at(d),
             device_id_type=MESH,
         )
 
-    for d in sorted(range(1, NZC), key=lambda d: -min(d, NZC - d)):
+    for d in near:
         one(d).start()
+
+    def relay(start, goal, count, d):
+        return pltpu.make_async_remote_copy(
+            src_ref=column_buf.at[pl.ds(start, count)],
+            dst_ref=column_buf.at[pl.ds(goal, count)],
+            send_sem=send_one.at[1],
+            recv_sem=recv_one.at[1],
+            device_id=chip_at(d),
+            device_id_type=MESH,
+        )
 
     def drain(region, send_sem, recv_sem):
         return pltpu.make_async_remote_copy(
@@ -202,17 +220,20 @@
 
     lanes = lax.broadcasted_iota(jnp.int32, (8, PART), 1)
     for half in range(2):
-        count = 7 if half == 0 else 8
-        drain(column_buf.at[pl.ds(half * 8, count)], send_one, recv_one.at[half]).wait_recv()
+        taken = drain(column_buf.at[pl.ds(0, 8 - half)], send_one.at[half], recv_one.at[half])
+        taken.wait_recv()
+        if half == 0:
+            relay(4, 8, 4, NZC - REACH).start()
+            relay(0, 12, 3, REACH).start()
         wide = column_buf[half * 8 : (half + 1) * 8].reshape(8, ROW)
-        narrow = wide.astype(BF16)
-        lib[half, core, place, :, 0:ROW] = narrow
-        rest = wide - narrow.astype(F32)
+        rest = wide - wide.astype(BF16).astype(F32)
         tail = jnp.zeros((8, PART), F32)
         for n in range(9):
             lead = jnp.broadcast_to(rest[:, n * PART : n * PART + 1], (8, PART))
             tail = jnp.where(lanes == n, lead, tail)
-        lib[half, core, place, :, ROW:SLAB] = tail.astype(BF16)
+        ends = jnp.concatenate([wide[:, SPLIT:ROW], tail], axis=1)
+        pair = jnp.concatenate([wide[:, 0:SPLIT], ends], axis=0)
+        lib[half, core, place] = pair.astype(BF16)
         for d in range(1, NP):
             two(half, d).start()
 
@@ -228,7 +249,9 @@
             [lib[half, c, k * 4 + f] for half in range(2) for c in range(2) for k in range(4)],
             axis=0,
         )
-        chosen = jnp.dot(hot, part, preferred_element_type=F32)
+        chosen = jnp.concatenate(
+            [jnp.dot(pick, part, preferred_element_type=F32) for pick in hot], axis=1
+        )
         if f:
             blocks[f] = chosen[:, 0:ROW]
         else:
@@ -437,8 +460,9 @@
     for k, g in enumerate(taken + now):
         weights_out[k][...] = jnp.broadcast_to(g, (1, PART))
 
-    drain(column_buf.at[pl.ds(0, NZC - 1)], send_one, recv_one.at[0]).wait_send()
     for half in range(2):
+        region = column_buf.at[pl.ds(0, 8 - half)]
+        drain(region, send_one.at[half], recv_one.at[half]).wait_send()
         region = lib.at[half, core, pl.ds(0, NP - 1)]
         drain(region, send_two.at[half], recv_two.at[half]).wait_send()
         three(half, core).wait_send()
@@ -466,14 +490,14 @@
             pltpu.VMEM((VOX, VOX), BF16),
             pltpu.VMEM((1, ROW), F32),
             pltpu.VMEM((NZC, 1, ROW), F32),
-            pltpu.VMEM((2, 2, NP, 8, SLAB), BF16),
+            pltpu.VMEM((2, 2, NP, 16, SPLIT), BF16),
             pltpu.VMEM((4, POINTS, ROW), F32),
             pltpu.VMEM((ITERS, 4 * FIELDS + 16, PART), F32),
             pltpu.VMEM((ITERS, 4 * FIELDS + 16, PART), F32),
             pltpu.VMEM((NP, 1, PART), F32),
             pltpu.VMEM((NGX, 1, PART), F32),
             dma((7,)),
-            dma,
+            dma((2,)),
             dma((2,)),
             dma((2,)),
             dma((2,)),

time: 58.2 us -> 57.4 us (0.986)
  Pallas kernels: 56.7 us -> 55.9 us
    pallas_call x1, Pallas kernels: 56.7 us -> 55.9 us  [per_device(): pl.pallas_call(kernel, out_shape=[jax.ShapeDtypeStruct((FIELDS * 8, PART)...]
where the time goes in v3:
time: 57.4 us; the launch traced here: 57.2 us
  Pallas kernels  55.9 us (97%)
  other arithmetic  0.72 us (1%)
  between operations  0.64 us (1%)
    pallas_call x1, Pallas kernels, per_device(): pl.pallas_call(kernel, out_shape=[jax.ShapeDtypeStruct((FIELDS * 8, PART)...  55.9 us

profile of v3, /device:TPU:1, one launch (start us, length us, event | category | flops | bytes accessed | tf_op | source)
XLA Modules:
  0.0 57.2 jit_solution(12942305211606350441)
XLA Ops:
  0.6 55.9 %shard_map.86 = (f32[192,128]{1,0:T(8,128)S(1)}, f32[192,128]{1,0:T(8,128)S(1)}, f32[192,128]{1,0:T(8,128)S(1)}, f32[192,128]{1,0:T(8,128)S(1)}, f32[1,128]{1,0:...) custom-call(f32[3,8,8,128]{3,2,1,0:T(8,128)} %source_hbm.1, ...), custom_call_target="tpu_custom_call" | custom-call | tf_op jit(solution)/shard_map/pallas_call | solution.py:477
  56.5 0.7 %multiply_add_fusion = (f32[3,8,8,128]{3,2,1,0:T(8,128)}, f32[3,8,8,128]{3,2,1,0:T(8,128)}) fusion(f32[3,8,8,128]{3,2,1,0:T(8,128)S(1)} %bitcast.19, f32[3,8,8,128]{3,2,1,0:T(8,128)S(1)} %bitcast.18, f32[3,8,8,128]{3,2,1,0:T(8,128)S(1)} %bitcast.17, f32[3,8,8,128]{3,2,1,0:T(8,128)S(1)} %bitcast.16, f32[128]{0:T(128)S(1)} %bitcast.26, f32[128]{0:T(128)S(1)} %bitcast.25, ...), kind=kLoop, calls=%fused_computation | loop fusion | flops 294912 | bytes 593408 | tf_op jit(solution)/shard_map/add | solution.py:532

commit v4 on v3

--- a/solution.py
+++ b/solution.py
@@ -19,6 +19,10 @@
 NP = 16
 OWN = 3
 REACH = 4
+WIDE = 56
+IN_XY = 4 * WIDE + 32
+IN_XZ = IN_XY + 4 * 24
+IN_YZ = IN_XZ + 32
 PART = 128
 ROW = 9 * PART
 SLAB = ROW + PART
@@ -76,6 +80,8 @@
     blocks,
     out_halo,
     in_halo,
+    wide_out,
+    wide_in,
     plane_buf,
     line_buf,
     load_sems,
@@ -87,6 +93,8 @@
     recv_three,
     send_halo,
     recv_halo,
+    send_wide,
+    recv_wide,
     send_sum,
     recv_sum,
 ):
@@ -99,8 +107,18 @@
     def on_line(target):
         return {"gx": target, "gy": gy, "gz": gz}
 
-    def on_plane(target):
-        return {"gx": gx, "gy": target // 4, "gz": target % 4}
+    def ring(d):
+        return min(d, 4 - d)
+
+    plane_steps = sorted(
+        range(1, NP), key=lambda d: (-ring(d // 4) - ring(d % 4), d)
+    )
+
+    def plane_at(d):
+        return {"gx": gx, "gy": lax.rem(gy + d // 4, 4), "gz": lax.rem(gz + d % 4, 4)}
+
+    def opposite(d):
+        return (4 - d // 4) % 4 * 4 + (4 - d % 4) % 4
 
     barrier = pltpu.get_barrier_semaphore()
     near = [d for reach in range(REACH, 0, -1) for d in (reach, NZC - reach)]
@@ -110,10 +128,8 @@
 
     for d in near:
         pl.semaphore_signal(barrier, inc=1, device_id=chip_at(d), device_id_type=MESH)
-    for d in range(1, NP):
-        pl.semaphore_signal(
-            barrier, inc=1, device_id=on_plane(lax.rem(place + d, NP)), device_id_type=MESH
-        )
+    for d in plane_steps:
+        pl.semaphore_signal(barrier, inc=1, device_id=plane_at(d), device_id_type=MESH)
     pl.semaphore_signal(
         barrier, inc=1, device_id=on_line(chip * 2 + 1 - core), device_id_type=MESH
     )
@@ -142,6 +158,21 @@
     for n in range(9):
         slice_buf[:, n * PART : (n + 1) * PART] = inverse_ref[n, pl.ds(gy, 1), :]
     column_buf[OWN] = slice_buf[...]
+
+    pl.semaphore_wait(barrier, 2 * REACH + NP)
+
+    def one(d):
+        return pltpu.make_async_remote_copy(
+            src_ref=slice_buf,
+            dst_ref=column_buf.at[(OWN - d) % NZC],
+            send_sem=send_one.at[0],
+            recv_sem=recv_one.at[0],
+            device_id=chip_at(d),
+            device_id_type=MESH,
+        )
+
+    for d in near:
+        one(d).start()
 
     for load in loads[1:]:
         load.wait()
@@ -169,21 +200,6 @@
 
     first = spectrum_of([(weights[i] * base[i]).astype(BF16) for i in range(3)])
 
-    pl.semaphore_wait(barrier, 2 * REACH + NP)
-
-    def one(d):
-        return pltpu.make_async_remote_copy(
-            src_ref=slice_buf,
-            dst_ref=column_buf.at[(OWN - d) % NZC],
-            send_sem=send_one.at[0],
-            recv_sem=recv_one.at[0],
-            device_id=chip_at(d),
-            device_id_type=MESH,
-        )
-
-    for d in near:
-        one(d).start()
-
     def relay(start, goal, count, d):
         return pltpu.make_async_remote_copy(
             src_ref=column_buf.at[pl.ds(start, count)],
@@ -211,7 +227,7 @@
             dst_ref=at,
             send_sem=send_two.at[half],
             recv_sem=recv_two.at[half],
-            device_id=on_plane(lax.rem(place + d, NP)),
+            device_id=plane_at(d),
             device_id_type=MESH,
         )
 
@@ -234,7 +250,7 @@
         ends = jnp.concatenate([wide[:, SPLIT:ROW], tail], axis=1)
         pair = jnp.concatenate([wide[:, 0:SPLIT], ends], axis=0)
         lib[half, core, place] = pair.astype(BF16)
-        for d in range(1, NP):
+        for d in plane_steps:
             two(half, d).start()
 
     for half in range(2):
@@ -345,25 +361,198 @@
     ]
     moments = []
 
-    for step in range(ITERS):
+    def around(dx, dy, dz):
+        return {
+            "gx": lax.rem(gx + dx + NGX, NGX),
+            "gy": lax.rem(gy + dy + 4, 4),
+            "gz": lax.rem(gz + dz + 4, 4),
+        }
+
+    ends = (-1, 1)
+    inside = [
+        [jnp.where(edge, 0.0, 1.0) for edge in pair]
+        for pair in ((gx == 0, gx == NGX - 1), (gy == 0, gy == 3), (gz == 0, gz == 3))
+    ]
+
+    def turn_faces(values, first, last):
+        faces = jnp.zeros((8, PART), F32)
+        for n, value in enumerate(values):
+            at_low = pltpu.roll(value, (2 * n + 1 + last) % PART, 1)
+            at_high = at_low
+            if first or last:
+                at_high = pltpu.roll(value, (2 * n + 1 - first) % PART, 1)
+            faces = jnp.where(lane == 2 * n, at_low, jnp.where(lane == 2 * n + 1, at_high, faces))
+        return faces
+
+    def start_wide(group):
+        rows, lines, edges, faces = [], [], [], []
+        for e in range(2):
+            o = 1 - e
+            lines.append((e * WIDE, WIDE, o * WIDE, around(ends[e], 0, 0)))
+            lines.append(((2 + e) * WIDE, WIDE, (2 + o) * WIDE, around(0, ends[e], 0)))
+            faces.append((4 * WIDE, 16, 4 * WIDE + 16 * o, around(0, 0, ends[e])))
+        for e in range(2):
+            for g in range(2):
+                slot = (1 - e) * 2 + 1 - g
+                rows.append(
+                    ((2 + g) * WIDE, FIELDS, IN_XY + slot * FIELDS, around(ends[e], ends[g], 0))
+                )
+                edges.append((4 * WIDE, 8, IN_XZ + slot * 8, around(ends[e], 0, ends[g])))
+                edges.append((4 * WIDE, 8, IN_YZ + slot * 8, around(0, ends[e], ends[g])))
+        for origin, size, goal, target in (rows, lines, edges, faces)[group]:
+            pltpu.make_async_remote_copy(
+                src_ref=wide_out.at[pl.ds(origin, size)],
+                dst_ref=wide_in.at[pl.ds(goal, size)],
+                send_sem=send_wide,
+                recv_sem=recv_wide,
+                device_id=target,
+                device_id_type=MESH,
+            ).start()
+
+    def send_wide_halo():
+        for e, (near_y, next_y) in enumerate(((0, 1), (7, 6))):
+            at = (2 + e) * WIDE
+            wide_out[at : at + 24, :] = basis[0][pl.ds(near_y, FIELDS, stride=8), :]
+            wide_out[at + 24 : at + 48, :] = basis[0][pl.ds(next_y, FIELDS, stride=8), :]
+            wide_out[at + 48 : at + 56, :] = jnp.broadcast_to(
+                diagonal[near_y : near_y + 1], (8, PART)
+            )
+        start_wide(0)
+        for e, (near_x, next_x) in enumerate(((0, 1), (7, 6))):
+            at = e * WIDE
+            for c in range(3):
+                wide_out[at + c * 8 : at + c * 8 + 8, :] = tile(0, c * 8 + near_x)
+                wide_out[at + 24 + c * 8 : at + 32 + c * 8, :] = tile(0, c * 8 + next_x)
+            wide_out[at + 48 : at + 56, :] = diagonal
+        start_wide(1)
+        values = [tile(0, n) for n in range(FIELDS)]
+        wide_out[4 * WIDE : 4 * WIDE + 8, :] = turn_faces(values + [diagonal], 0, 0)
+        start_wide(2)
+        wide_out[4 * WIDE + 8 : 4 * WIDE + 16, :] = turn_faces(values, 1, 1)
+        start_wide(3)
+
+    def spread_row(value):
+        return jnp.broadcast_to(value, (8, PART))
+
+    def image_on_faces():
+        even = lane % 2 == 0
+
+        def part(at, size=8):
+            return wide_in[at : at + size, :]
+
+        def corner_rows(e, g, n):
+            at = IN_XY + (e * 2 + g) * FIELDS + n
+            return wide_in[at : at + 1, :] * inside[0][e] * inside[1][g]
+
+        def mixed(at, low, high):
+            return jnp.where(even, part(at) * low, part(at + 8) * high)
+
+        xz = [mixed(IN_XZ + 16 * e, *inside[2]) * inside[0][e] for e in range(2)]
+        yz = [mixed(IN_YZ + 16 * e, *inside[2]) * inside[1][e] for e in range(2)]
+        for e in range(2):
+            n_at = 7 if e == 0 else 0
+            at = e * WIDE
+            own_x = 0 if e == 0 else 7
+            for c in range(3):
+                value = part(at + c * 8)
+                n = c * 8 + n_at
+                beside = part(at + 24 + c * 8) + tile(0, c * 8 + own_x)
+                beside = beside + jnp.where(
+                    sub == 0, spread_row(corner_rows(e, 0, n)), pltpu.roll(value, 1, 0)
+                )
+                beside = beside + jnp.where(
+                    sub == 7, spread_row(corner_rows(e, 1, n)), pltpu.roll(value, 7, 0)
+                )
+                beside = beside + jnp.where(
+                    lane == 0,
+                    pltpu.roll(xz[e], (PART - 2 * n) % PART, 1),
+                    pltpu.roll(value, 1, 1),
+                )
+                beside = beside + jnp.where(
+                    lane == PART - 1,
+                    pltpu.roll(xz[e], (PART - 2 - 2 * n) % PART, 1),
+                    pltpu.roll(value, PART - 1, 1),
+                )
+                image = part(at + 48) * value - THETA * beside
+                goal = starts[e] + c * 8
+                in_halo[1, goal : goal + 8, :] = image * inside[0][e]
+            at = (2 + e) * WIDE
+            row_at = 7 if e == 0 else 0
+            edge = spread_row(yz[e][row_at : row_at + 1])
+            for c in range(3):
+                value = part(at + c * 8)
+                own = wide_out[at + c * 8 : at + c * 8 + 8, :]
+                beside = part(at + 24 + c * 8) + own
+                beside = beside + jnp.where(
+                    sub == 0, spread_row(corner_rows(0, e, c * 8 + 7)), pltpu.roll(value, 1, 0)
+                )
+                beside = beside + jnp.where(
+                    sub == 7, spread_row(corner_rows(1, e, c * 8)), pltpu.roll(value, 7, 0)
+                )
+                lanes_low = 2 * (c * 8 + sub)
+                low = jnp.sum(jnp.where(lane == lanes_low, edge, 0.0), axis=1, keepdims=True)
+                high = jnp.sum(jnp.where(lane == lanes_low + 1, edge, 0.0), axis=1, keepdims=True)
+                beside = beside + jnp.where(
+                    lane == 0, jnp.broadcast_to(low, (8, PART)), pltpu.roll(value, 1, 1)
+                )
+                beside = beside + jnp.where(
+                    lane == PART - 1,
+                    jnp.broadcast_to(high, (8, PART)),
+                    pltpu.roll(value, PART - 1, 1),
+                )
+                image = part(at + 48) * value - THETA * beside
+                goal = starts[2 + e] + c * 8
+                in_halo[1, goal : goal + 8, :] = image * inside[1][e]
+        at = 4 * WIDE
+        value = jnp.where(even, part(at), part(at + 16))
+        beyond = jnp.where(even, part(at + 8), part(at + 24))
+        faces = wide_out[at : at + 8, :]
+        own = jnp.where(even, pltpu.roll(faces, PART - 1, 1), pltpu.roll(faces, 1, 1))
+        weight = jnp.where(
+            even,
+            jnp.broadcast_to(part(at)[:, 48:49], (8, PART)),
+            jnp.broadcast_to(part(at + 16)[:, 49:50], (8, PART)),
+        )
+        beside = beyond + own
+        beside = beside + jnp.where(
+            sub == 0, pltpu.roll(yz[0], 1, 0), pltpu.roll(value, 1, 0)
+        )
+        beside = beside + jnp.where(
+            sub == 7, pltpu.roll(yz[1], 7, 0), pltpu.roll(value, 7, 0)
+        )
+        spot = lane // 2 % 8
+        beside = beside + jnp.where(
+            spot == 0, pltpu.roll(xz[0], PART - 14, 1), pltpu.roll(value, 2, 1)
+        )
+        beside = beside + jnp.where(
+            spot == 7, pltpu.roll(xz[1], 14, 1), pltpu.roll(value, PART - 2, 1)
+        )
+        image = weight * value - THETA * beside
+        in_halo[1, starts[4] : starts[4] + 8, :] = image
+        in_halo[1, starts[5] : starts[5] + 8, :] = image
+
+    def send_halo_of(step):
         for c in range(3):
             at = c * 8
             out_halo[step, starts[0] + at : starts[0] + at + 8, :] = tile(step, at)
             out_halo[step, starts[1] + at : starts[1] + at + 8, :] = tile(step, at + 7)
         halo(step, 0).start()
         halo(step, 1).start()
-        faces = jnp.zeros((8, PART), F32)
-        for n in range(FIELDS):
-            turned = pltpu.roll(tile(step, n), 2 * n + 1, 1)
-            faces = jnp.where(lane // 2 == n, turned, faces)
+        out_halo[step, starts[2] : starts[3], :] = basis[step][pl.ds(0, FIELDS, stride=8), :]
+        out_halo[step, starts[3] : starts[4], :] = basis[step][pl.ds(7, FIELDS, stride=8), :]
+        halo(step, 2).start()
+        halo(step, 3).start()
+        faces = turn_faces([tile(step, n) for n in range(FIELDS)], 0, 0)
         out_halo[step, starts[4] : starts[4] + 8, :] = faces
         out_halo[step, starts[5] : starts[5] + 8, :] = faces
         halo(step, 4).start()
         halo(step, 5).start()
-        out_halo[step, starts[2] : starts[3], :] = basis[step][pl.ds(0, FIELDS, stride=8), :]
-        out_halo[step, starts[3] : starts[4], :] = basis[step][pl.ds(7, FIELDS, stride=8), :]
-        halo(step, 2).start()
-        halo(step, 3).start()
+
+    for step in range(ITERS):
+        if step == 0:
+            send_wide_halo()
+        if step == 2:
+            send_halo_of(step)
         for n in range(FIELDS):
             value = tile(step, n)
             beside = jnp.where(sub == 0, 0.0, pltpu.roll(value, 1, 0))
@@ -375,25 +564,36 @@
             if n % 8 < 7:
                 beside = beside + tile(step, n + 1)
             basis[step + 1][n * 8 : (n + 1) * 8, :] = diagonal * value - THETA * beside
-        if step:
-            moments.append(dot(step - 1, step))
-        moments.append(dot(step, step))
-        drain(in_halo.at[step], send_halo, recv_halo.at[step]).wait_recv()
-        low = in_halo[step, starts[4] : starts[4] + 8, :] * keep[4]
-        high = in_halo[step, starts[5] : starts[5] + 8, :] * keep[5]
+        if step == 0:
+            moments.append(dot(0, 0))
+            drain(wide_in, send_wide, recv_wide).wait_recv()
+            image_on_faces()
+        if step == 2:
+            moments.extend((dot(0, 1), dot(1, 1), dot(1, 2), dot(2, 2)))
+            drain(in_halo.at[step], send_halo, recv_halo.at[step]).wait_recv()
+
+        def face(side, at=0, size=8):
+            if step == 0:
+                if side < 4:
+                    return wide_in[side * WIDE + at : side * WIDE + at + size, :]
+                return wide_in[4 * WIDE + (side - 4) * 16 : 4 * WIDE + (side - 4) * 16 + 8, :]
+            return in_halo[step, starts[side] + at : starts[side] + at + size, :]
+
+        low = face(4) * keep[4]
+        high = face(5) * keep[5]
         both = jnp.where(lane % 2 == 0, low, pltpu.roll(high, PART - 2, 1))
         for n in range(FIELDS):
             turned = pltpu.roll(both, (PART - 2 * n) % PART, 1)
             more = jnp.where((lane == 0) | (lane == PART - 1), turned, 0.0)
-            row_low = in_halo[step, starts[2] + n : starts[2] + n + 1, :] * keep[2]
-            row_high = in_halo[step, starts[3] + n : starts[3] + n + 1, :] * keep[3]
+            row_low = face(2, n, 1) * keep[2]
+            row_high = face(3, n, 1) * keep[3]
             more = more + jnp.where(sub == 0, jnp.broadcast_to(row_low, (8, PART)), 0.0)
             more = more + jnp.where(sub == 7, jnp.broadcast_to(row_high, (8, PART)), 0.0)
             at = n // 8 * 8
             if n % 8 == 0:
-                more = more + in_halo[step, starts[0] + at : starts[0] + at + 8, :] * keep[0]
+                more = more + face(0, at) * keep[0]
             if n % 8 == 7:
-                more = more + in_halo[step, starts[1] + at : starts[1] + at + 8, :] * keep[1]
+                more = more + face(1, at) * keep[1]
             basis[step + 1][n * 8 : (n + 1) * 8, :] += more
     moments.append(dot(ITERS - 1, ITERS))
 
@@ -402,28 +602,37 @@
     for k, moment in enumerate(moments):
         packed = jnp.where(row == k, moment, packed)
 
-    def all_sum(value, buf, n, turn, device_of):
+    def all_sum(value, buf, n, turn, steps, slot_of, device_of):
         buf[0] = value
 
         def copy(d):
             return pltpu.make_async_remote_copy(
                 src_ref=buf.at[0],
-                dst_ref=buf.at[n - d],
+                dst_ref=buf.at[slot_of(d)],
                 send_sem=send_sum.at[turn],
                 recv_sem=recv_sum.at[turn],
                 device_id=device_of(d),
                 device_id_type=MESH,
             )
 
-        for d in sorted(range(1, n), key=lambda d: -min(d, n - d)):
+        for d in steps:
             copy(d).start()
         arrived = drain(buf.at[pl.ds(1, n - 1)], send_sum.at[turn], recv_sum.at[turn])
         arrived.wait_recv()
         return jnp.sum(buf[...], axis=0)
 
-    packed = all_sum(packed, plane_buf, NP, 0, lambda d: on_plane(lax.rem(place + d, NP)))
-    total = all_sum(packed, line_buf, NGX, 1, lambda d: on_line(lax.rem(gx + d, NGX)))
-    m = [total[:, k : k + 1] for k in range(6)]
+    line_steps = sorted(range(1, NGX), key=lambda d: -min(d, NGX - d))
+    packed = all_sum(packed, plane_buf, NP, 0, plane_steps, opposite, plane_at)
+    total = all_sum(
+        packed,
+        line_buf,
+        NGX,
+        1,
+        line_steps,
+        lambda d: NGX - d,
+        lambda d: on_line(lax.rem(gx + d, NGX)),
+    )
+    m = [jnp.broadcast_to(total[:, k : k + 1], (1, PART)) for k in range(6)]
 
     def product(a, b):
         result = None
@@ -433,7 +642,7 @@
                 result = term if result is None else result + term
         return result
 
-    unit = jnp.ones((1, 1), F32)
+    unit = jnp.ones((1, PART), F32)
     now = [unit]
     course = [unit]
     taken = []
@@ -458,7 +667,7 @@
             ]
             norm = following
     for k, g in enumerate(taken + now):
-        weights_out[k][...] = jnp.broadcast_to(g, (1, PART))
+        weights_out[k][...] = g
 
     for half in range(2):
         region = column_buf.at[pl.ds(0, 8 - half)]
@@ -466,7 +675,8 @@
         region = lib.at[half, core, pl.ds(0, NP - 1)]
         drain(region, send_two.at[half], recv_two.at[half]).wait_send()
         three(half, core).wait_send()
-    drain(out_halo, send_halo, recv_halo.at[0]).wait_send()
+    drain(out_halo.at[2], send_halo, recv_halo.at[2]).wait_send()
+    drain(wide_in, send_wide, recv_wide).wait_send()
     drain(plane_buf.at[pl.ds(1, NP - 1)], send_sum.at[0], recv_sum.at[0]).wait_send()
     drain(line_buf.at[pl.ds(1, NGX - 1)], send_sum.at[1], recv_sum.at[1]).wait_send()
 
@@ -494,6 +704,8 @@
             pltpu.VMEM((4, POINTS, ROW), F32),
             pltpu.VMEM((ITERS, 4 * FIELDS + 16, PART), F32),
             pltpu.VMEM((ITERS, 4 * FIELDS + 16, PART), F32),
+            pltpu.VMEM((4 * WIDE + 16, PART), F32),
+            pltpu.VMEM((IN_YZ + 32, PART), F32),
             pltpu.VMEM((NP, 1, PART), F32),
             pltpu.VMEM((NGX, 1, PART), F32),
             dma((7,)),
@@ -505,6 +717,8 @@
             dma((2,)),
             dma,
             dma((ITERS,)),
+            dma,
+            dma,
             dma((2,)),
             dma((2,)),
         ],

time: 57.4 us -> 54.7 us (0.953)
  Pallas kernels: 55.9 us -> 53.2 us
    pallas_call x1, Pallas kernels: 55.9 us -> 53.2 us  [per_device(): pl.pallas_call(kernel, out_shape=[jax.ShapeDtypeStruct((FIELDS * 8, PART)...]
where the time goes in v4:
time: 54.7 us; the launch traced here: 54.6 us
  Pallas kernels  53.2 us (97%)
  other arithmetic  0.72 us (1%)
  between operations  0.64 us (1%)
    pallas_call x1, Pallas kernels, per_device(): pl.pallas_call(kernel, out_shape=[jax.ShapeDtypeStruct((FIELDS * 8, PART)...  53.2 us

profile of v4, /device:TPU:1, one launch (start us, length us, event | category | flops | bytes accessed | tf_op | source)
XLA Modules:
  0.0 54.6 jit_solution(2630253920460549837)
XLA Ops:
  0.6 53.2 %shard_map.86 = (f32[192,128]{1,0:T(8,128)S(1)}, f32[192,128]{1,0:T(8,128)S(1)}, f32[192,128]{1,0:T(8,128)S(1)}, f32[192,128]{1,0:T(8,128)S(1)}, f32[1,128]{1,0:...) custom-call(f32[3,8,8,128]{3,2,1,0:T(8,128)} %source_hbm.1, ...), custom_call_target="tpu_custom_call" | custom-call | tf_op jit(solution)/shard_map/pallas_call | solution.py:687
  53.8 0.7 %multiply_add_fusion = (f32[3,8,8,128]{3,2,1,0:T(8,128)}, f32[3,8,8,128]{3,2,1,0:T(8,128)}) fusion(f32[3,8,8,128]{3,2,1,0:T(8,128)S(1)} %bitcast.19, f32[3,8,8,128]{3,2,1,0:T(8,128)S(1)} %bitcast.18, f32[3,8,8,128]{3,2,1,0:T(8,128)S(1)} %bitcast.17, f32[3,8,8,128]{3,2,1,0:T(8,128)S(1)} %bitcast.16, f32[128]{0:T(128)S(1)} %bitcast.26, f32[128]{0:T(128)S(1)} %bitcast.25, ...), kind=kLoop, calls=%fused_computation | loop fusion | flops 294912 | bytes 593408 | tf_op jit(solution)/shard_map/add | solution.py:746

commit v5 on v4

--- a/solution.py
+++ b/solution.py
@@ -622,8 +622,7 @@
         return jnp.sum(buf[...], axis=0)
 
     line_steps = sorted(range(1, NGX), key=lambda d: -min(d, NGX - d))
-    packed = all_sum(packed, plane_buf, NP, 0, plane_steps, opposite, plane_at)
-    total = all_sum(
+    packed = all_sum(
         packed,
         line_buf,
         NGX,
@@ -632,6 +631,7 @@
         lambda d: NGX - d,
         lambda d: on_line(lax.rem(gx + d, NGX)),
     )
+    total = all_sum(packed, plane_buf, NP, 0, plane_steps, opposite, plane_at)
     m = [jnp.broadcast_to(total[:, k : k + 1], (1, PART)) for k in range(6)]
 
     def product(a, b):

time: 54.7 us -> 53.9 us (0.985)
  Pallas kernels: 53.2 us -> 52.4 us
    pallas_call x1, Pallas kernels: 53.2 us -> 52.4 us  [per_device(): pl.pallas_call(kernel, out_shape=[jax.ShapeDtypeStruct((FIELDS * 8, PART)...]
where the time goes in v5:
time: 53.9 us; the launch traced here: 53.7 us
  Pallas kernels  52.4 us (97%)
  other arithmetic  0.72 us (1%)
  between operations  0.64 us (1%)
    pallas_call x1, Pallas kernels, per_device(): pl.pallas_call(kernel, out_shape=[jax.ShapeDtypeStruct((FIELDS * 8, PART)...  52.4 us

profile of v5, /device:TPU:1, one launch (start us, length us, event | category | flops | bytes accessed | tf_op | source)
XLA Modules:
  0.0 53.7 jit_solution(3836155698555860856)
XLA Ops:
  0.6 52.4 %shard_map.86 = (f32[192,128]{1,0:T(8,128)S(1)}, f32[192,128]{1,0:T(8,128)S(1)}, f32[192,128]{1,0:T(8,128)S(1)}, f32[192,128]{1,0:T(8,128)S(1)}, f32[1,128]{1,0:...) custom-call(f32[3,8,8,128]{3,2,1,0:T(8,128)} %source_hbm.1, ...), custom_call_target="tpu_custom_call" | custom-call | tf_op jit(solution)/shard_map/pallas_call | solution.py:687
  53.0 0.7 %multiply_add_fusion = (f32[3,8,8,128]{3,2,1,0:T(8,128)}, f32[3,8,8,128]{3,2,1,0:T(8,128)}) fusion(f32[3,8,8,128]{3,2,1,0:T(8,128)S(1)} %bitcast.19, f32[3,8,8,128]{3,2,1,0:T(8,128)S(1)} %bitcast.18, f32[3,8,8,128]{3,2,1,0:T(8,128)S(1)} %bitcast.17, f32[3,8,8,128]{3,2,1,0:T(8,128)S(1)} %bitcast.16, f32[128]{0:T(128)S(1)} %bitcast.26, f32[128]{0:T(128)S(1)} %bitcast.25, ...), kind=kLoop, calls=%fused_computation | loop fusion | flops 294912 | bytes 593408 | tf_op jit(solution)/shard_map/add | solution.py:746
